TPU v7x, 32 devices: a whole 2x2x4 slice. The times are simulated.
32 devices in a mesh: exp: 8 (over z, x), head: 4 (over y, core).
Axes of the slice: x: 2, y: 2, z: 4, core: 2. Of those that a mesh axis runs over, the one named last changes fastest.
Arguments:
- queries: bfloat16 [1024, 4096], P('exp', 'head')
- keys: bfloat16 [1024, 1024], P('exp', 'head')
- values: bfloat16 [1024, 1024], P('exp', 'head')
- w_in: bfloat16 [8, 4096, 2, 768], P('exp', 'head'), may hold values from -0.09375 to 0.09375
- w_out: bfloat16 [8, 768, 4096], P('exp', None, 'head'), may hold values from -0.21875 to 0.21875
- routes: int32 [1024, 6], P('exp'), may hold values from 0 to 7, as said below
- route_weights: float32 [1024, 6], P('exp'), may hold values from 0.05 to 0.45
- grad_out: bfloat16 [1024, 4096], P('exp', 'head'), may hold values from -6 to 6
Outputs:
- output: bfloat16 [1024, 4096], P('exp', 'head')
- grad_attended: bfloat16 [1024, 4096], P('exp', 'head')
Inputs may be any that keep to these rules, and one draw needn't show every extreme that they name: `routes`: each row names 6 different experts. In each aligned block of 128 rows (the rows of one index of exp) no expert is named more than 112 times.
All inputs are finite; a program needn't handle non-finite values.
Results may differ from a plain program's by a relative error of at most 0.017.
Values may be sent and summed in bfloat16 or wider, within the bound.
A program may use at most 128 MiB of HBM per device.

v0:
```python
import jax
import jax.numpy as jnp
from jax import lax
from jax.sharding import PartitionSpec as P

D = 4096
HEAD_WIDTH = 128
TOP = 6


norm_eps = 1e-05
hidden_logits = -1e30


def block_partial(query_rows, query_pos, rows_of_keys, value_rows, key_pos):
    row_count = query_rows.shape[0]
    count_of_blocks = rows_of_keys.shape[0]
    kv_heads = rows_of_keys.shape[2] // HEAD_WIDTH
    grouping_width = query_rows.shape[1] // HEAD_WIDTH // kv_heads
    heads_of_queries = query_rows.reshape(row_count, kv_heads, grouping_width, HEAD_WIDTH)
    key_heads = rows_of_keys.reshape(count_of_blocks, -1, kv_heads, HEAD_WIDTH)
    value_heads = value_rows.reshape(count_of_blocks, -1, kv_heads, HEAD_WIDTH)
    visible = (key_pos[:, None, :] <= query_pos[None, :, None])[:, :, None, None, :]
    scores = jnp.einsum(
        "tgid,bjgd->btgij", heads_of_queries, key_heads, preferred_element_type=jnp.float32
    ) * HEAD_WIDTH ** (-0.5)
    scores = jnp.where(visible, scores, hidden_logits)
    best_score = jnp.max(scores, axis=-1).astype(jnp.bfloat16)
    weights = jnp.where(visible, jnp.exp(scores - best_score.astype(jnp.float32)[..., None]), 0.0)
    weight_total = jnp.sum(weights, axis=-1).astype(jnp.bfloat16)
    weighted_sum = jnp.einsum(
        "btgij,bjgd->btgid",
        weights.astype(jnp.bfloat16),
        value_heads,
        preferred_element_type=jnp.float32,
    ).astype(jnp.bfloat16)
    head_count = kv_heads * grouping_width
    return (
        best_score.reshape(count_of_blocks, row_count, head_count),
        weight_total.reshape(count_of_blocks, row_count, head_count),
        weighted_sum.reshape(count_of_blocks, row_count, head_count * HEAD_WIDTH),
    )


def fold_partials(running, best_score, weight_total, weighted_sum):
    top_now, total_now, sums_now = running
    best_value = best_score.astype(jnp.float32)
    new_top = jnp.maximum(top_now, jnp.max(best_value, axis=0))
    old_factor = jnp.exp(top_now - new_top)
    block_factor = jnp.exp(best_value - new_top[None])
    total_next = total_now * old_factor + jnp.sum(
        weight_total.astype(jnp.float32) * block_factor, axis=0
    )
    spread_sums = weighted_sum.reshape(
        weighted_sum.shape[0], sums_now.shape[0], sums_now.shape[1], HEAD_WIDTH
    )
    sums_next = sums_now * old_factor[..., None] + jnp.sum(
        spread_sums.astype(jnp.float32) * block_factor[..., None], axis=0
    )
    return (new_top, total_next, sums_next)


def per_device(queries, keys, values, w_in, w_out, routes, route_weights, grad_out):
    exp_count = lax.axis_size("exp")
    exp_index = lax.axis_index("exp")
    head_devices = lax.axis_size("head")
    token_count = queries.shape[0]
    query_width = queries.shape[1]
    head_count = query_width // HEAD_WIDTH
    cache_rows = keys.shape[0]
    window = token_count * exp_count
    offset = cache_rows * exp_count - window
    beginning = (
        jnp.full((token_count, head_count), hidden_logits, jnp.float32),
        jnp.zeros((token_count, head_count), jnp.float32),
        jnp.zeros((token_count, head_count, HEAD_WIDTH), jnp.float32),
    )
    own_pos = offset + exp_index * token_count + jnp.arange(token_count, dtype=jnp.int32)
    key_piece = lax.all_gather(keys, "exp", axis=0, tiled=True)
    value_piece = lax.all_gather(values, "exp", axis=0, tiled=True)
    piece_blocks = key_piece.shape[0] // cache_rows
    key_split = key_piece.reshape(piece_blocks, cache_rows, -1)
    value_split = value_piece.reshape(piece_blocks, cache_rows, -1)
    pos_split = jnp.arange(key_piece.shape[0], dtype=jnp.int32).reshape(piece_blocks, cache_rows)

    def one_block(state, element):
        key_block, value_block, pos_block = element
        block_parts = block_partial(
            queries, own_pos, key_block[None], value_block[None], pos_block[None]
        )
        return (fold_partials(state, block_parts[0], block_parts[1], block_parts[2]), None)

    state, ignored = lax.scan(one_block, beginning, (key_split, value_split, pos_split))
    attended = (
        (state[2] / state[1][..., None]).reshape(token_count, query_width).astype(jnp.bfloat16)
    )
    row_width = attended.shape[1]
    experts_all = w_in.shape[0] * exp_count
    mean_load = TOP * token_count // experts_all
    capacity = mean_load + mean_load // 6
    places = experts_all * capacity
    flat_routes = routes.reshape(-1)
    expert_hits = (
        flat_routes[:, None] == jnp.arange(experts_all, dtype=jnp.int32)[None, :]
    ).astype(jnp.int32)
    earlier = jnp.cumsum(expert_hits, axis=0) - expert_hits
    slot_index = jnp.sum(earlier * expert_hits, axis=1)
    place_index = flat_routes * capacity + slot_index
    chosen = (place_index[:, None] == jnp.arange(places, dtype=jnp.int32)[None, :]).astype(
        jnp.bfloat16
    )
    picker = jnp.sum(chosen.reshape(token_count, TOP, places), axis=1)
    contract_rows = (((0,), (0,)), ((), ()))
    send_rows = lax.dot_general(picker, attended, contract_rows, preferred_element_type=jnp.float32)
    send_rows = send_rows.astype(jnp.bfloat16).reshape(experts_all, capacity, row_width)
    send_grads = lax.dot_general(
        picker, grad_out, contract_rows, preferred_element_type=jnp.float32
    )
    send_grads = send_grads.astype(jnp.bfloat16).reshape(experts_all, capacity, row_width)
    w_first = w_in[0]
    w_second = w_out[0]
    rows_in = lax.all_to_all(send_rows, "exp", split_axis=0, concat_axis=0, tiled=True)
    grads_in = lax.all_to_all(send_grads, "exp", split_axis=0, concat_axis=0, tiled=True)
    lead_count, item_count, width_in = rows_in.shape
    row_total = lead_count * item_count
    row_block = rows_in.reshape(row_total, width_in)
    grad_block = grads_in.reshape(row_total, width_in)
    row_float = row_block.astype(jnp.float32)
    raw_sums = jnp.einsum("rd,dkf->rkf", row_block, w_first, preferred_element_type=jnp.float32)
    back_sums = lax.dot_general(
        grad_block, w_second, (((1,), (1,)), ((), ())), preferred_element_type=jnp.float32
    )
    squares = jnp.sum(row_float * row_float, axis=1)
    square_tile = jnp.broadcast_to(squares[:, None, None], (row_total, 1, head_devices))
    raw_part = lax.psum_scatter(raw_sums, "head", scatter_dimension=2, tiled=True)
    back_part = lax.psum_scatter(back_sums[:, None, :], "head", scatter_dimension=2, tiled=True)
    square_part = lax.psum_scatter(square_tile, "head", scatter_dimension=2, tiled=True)
    norm_scale = lax.rsqrt(square_part[:, 0] / D + norm_eps)
    gate_value = raw_part[:, 0] * norm_scale
    up_value = raw_part[:, 1] * norm_scale
    back_value = back_part[:, 0]
    gate_sigmoid = jax.nn.sigmoid(gate_value)
    gate_silu = gate_value * gate_sigmoid
    act_part = (gate_silu * up_value).astype(jnp.bfloat16)
    grad_gate = back_value * up_value * gate_sigmoid * (1.0 + gate_value * (1.0 - gate_sigmoid))
    grad_up = back_value * gate_silu
    grad_part = jnp.stack([grad_gate, grad_up], axis=1).astype(jnp.bfloat16)
    inner_part = jnp.sum(
        grad_part.astype(jnp.float32) * jnp.stack([gate_value, up_value], axis=1), axis=(1, 2)
    )
    act_whole = lax.all_gather(act_part[:, None, :], "head", axis=2, tiled=True)
    grad_hidden = lax.all_gather(grad_part, "head", axis=2, tiled=True)
    hidden_act = act_whole[:, 0]
    inner_sum = lax.psum(inner_part, "head")
    out_rows = jnp.dot(hidden_act, w_second, preferred_element_type=jnp.float32).astype(
        jnp.bfloat16
    )
    grad_normed = jnp.einsum(
        "rkf,dkf->rd", grad_hidden, w_first, preferred_element_type=jnp.float32
    )
    grad_rows = (
        norm_scale * grad_normed - row_float * (norm_scale * norm_scale / D) * inner_sum[:, None]
    )
    expert_out = out_rows.reshape(lead_count, item_count, width_in)
    expert_grad = grad_rows.astype(jnp.bfloat16).reshape(lead_count, item_count, width_in)
    came_out, came_grad = (
        lax.all_to_all(expert_out, "exp", split_axis=0, concat_axis=0, tiled=True),
        lax.all_to_all(expert_grad, "exp", split_axis=0, concat_axis=0, tiled=True),
    )
    picked_out = came_out.reshape(places, row_width)[place_index].reshape(
        token_count, TOP, row_width
    )
    picked_grad = came_grad.reshape(places, row_width)[place_index].reshape(
        token_count, TOP, row_width
    )
    output = attended.astype(jnp.float32) + jnp.sum(
        route_weights[:, :, None] * picked_out.astype(jnp.float32), axis=1
    )
    grad_attended = grad_out.astype(jnp.float32) + jnp.sum(
        route_weights[:, :, None] * picked_grad.astype(jnp.float32), axis=1
    )
    return (output.astype(jnp.bfloat16), grad_attended.astype(jnp.bfloat16))


def solution(mesh):
    in_specs = (
        P("exp", "head"),
        P("exp", "head"),
        P("exp", "head"),
        P("exp", "head", None, None),
        P("exp", None, "head"),
        P("exp", None),
        P("exp", None),
        P("exp", "head"),
    )
    out_specs = (P("exp", "head"), P("exp", "head"))
    return jax.shard_map(
        per_device, mesh=mesh, in_specs=in_specs, out_specs=out_specs, check_vma=False
    )
```

profile of v0, /device:TPU:0, one launch (start us, length us, event | category | flops | bytes accessed | tf_op | source)
XLA Modules:
  0.0 457.7 jit_solution(5686155765505619004)
XLA Ops:
  13.8 35.4 %all_gather.12 = bf16[1024,256]{1,0:T(8,128)(2,1)} all-gather(bf16[128,256]{1,0:T(8,128)(2,1)} %param.11), channel_id=1, replica_groups=mesh['exp'=8,'head'=4] {'exp'}, dimensions={0}, use_global_device_ids=true | all-gather | bytes 589824 | tf_op jit(solution)/shard_map/all_gather | solution.py:79
  49.3 33.6 %all_gather.13 = bf16[1024,256]{1,0:T(8,128)(2,1)} all-gather(bf16[128,256]{1,0:T(8,128)(2,1)} %param.12), channel_id=1, replica_groups=mesh['exp'=8,'head'=4] {'exp'}, dimensions={0}, use_global_device_ids=true | all-gather | bytes 589824 | tf_op jit(solution)/shard_map/all_gather | solution.py:80
  84.0 93.4 %while.16 = (s32[]{:T(128)}, f32[128,8]{0,1:T(8,128)}, f32[128,8]{0,1:T(8,128)}, f32[128,8,128]{0,2,1:T(8,128)}, s32[8,128]{1,0:T(8,128)}, /*index=5*/bf16[8,128...) while((s32[]{:T(128)}, f32[128,8]{0,1:T(8,128)}, ...), condition=%wide.wide.region_3.4_spmd.clone, body=%wide.wide.region_0.3_spmd.clone.sunk | while | flops 69099648 | bytes 4713100 | solution.py:93
  89.0 2.1 fusion.74
  100.6 2.1 fusion.74
  112.3 2.1 fusion.74
  124.0 2.1 fusion.74
  135.7 2.1 fusion.74
  147.4 2.1 fusion.74
  159.1 2.1 fusion.74
  170.7 2.1 fusion.74
  180.2 36.1 %all_to_all.20 = bf16[8,112,1024]{2,1,0:T(8,128)(2,1)S(1)} all-to-all(bf16[8,112,1024]{2,1,0:T(8,128)(2,1)S(1)} %bitcast.122), channel_id=1, replica_groups=mesh['exp'=8,'head'=4] {'exp'}, dimensions={0} | all-to-all | bytes 3670016 | tf_op jit(solution)/shard_map/all_to_all | solution.py:122
  217.7 5.3 %fusion.20 = f32[896,2,768]{0,2,1:T(8,128)} fusion(bf16[896,1024,1]{1,0,2:T(8,128)(2,1)S(1)} %bitcast.119, bf16[1024,2,768]{2,1,0:T(2,128)(2,1)S(1)} %bitcast.118), kind=kOutput, calls=%fused_computation.40 | convolution fusion | flops 2818572288 | bytes 10485760 | tf_op jit(solution)/shard_map/rd,dkf->rkf/dot_general | solution.py:129
  225.6 42.0 %all_to_all.21 = bf16[8,112,1024]{2,1,0:T(8,128)(2,1)S(1)} all-to-all(bf16[8,112,1024]{2,1,0:T(8,128)(2,1)S(1)} %bitcast.121), channel_id=1, replica_groups=mesh['exp'=8,'head'=4] {'exp'}, dimensions={0} | all-to-all | bytes 3670016 | tf_op jit(solution)/shard_map/all_to_all | solution.py:123
  267.6 3.3 convolution_bitcast_fusion
  274.2 10.1 %all-reduce = f32[896,1,4]{0,2,1:T(4,128)S(1)} all-reduce(f32[896,1,4]{0,2,1:T(4,128)S(1)} %broadcast_in_dim.43), channel_id=3, replica_groups=mesh['exp'=8,'head'=4] {'head'}, use_global_device_ids=true, to_apply=%region_10.11.clone | all-reduce | flops 3584 | bytes 28672
  285.1 2.8 multiply_convert_fusion.2
  288.0 25.3 %reduce-scatter.6.cloned.1.call-done = f32[896,1,192]{0,2,1:T(8,128)} async-done(((f32[896,1,768]{0,2,1:T(8,128)}), f32[896,1,192]{0,2,1:T(8,128)}) %reduce-scatter.6.cloned.1.call-update) | async-done | bytes 688144 | tf_op jit(solution)/shard_map/reduce_scatter | solution.py:136
  316.8 16.5 %all-gather.3.cloned.1.call-done = bf16[896,1,768]{0,2,1:T(8,128)(2,1)} async-done(((bf16[896,1,192]{0,2,1:T(8,128)(2,1)}), bf16[896,1,768]{0,2,1:T(8,128)(2,1)}) %all-gather.3.cloned.1.call-update) | async-done | bytes 1376272 | tf_op jit(solution)/shard_map/all_gather | solution.py:151
  333.3 4.7 %convolution_convert_fusion.1 = bf16[896,1024]{1,0:T(8,128)(2,1)} fusion(bf16[1,768,1024]{2,1,0:T(8,128)(2,1)} %param.14, bf16[896,1,768]{0,2,1:T(8,128)(2,1)} %all-gather.3.cloned.1.call-done), kind=kOutput, calls=%fused_computation.47 | convolution fusion | flops 1410203648 | bytes 4784128 | tf_op jit(solution)/shard_map/dot_general | solution.py:155
  338.0 5.5 %all-to-all-start.1 = ((bf16[8,112,1024]{2,1,0:T(8,128)(2,1)}), bf16[8,112,1024]{2,1,0:T(8,128)(2,1)}, u32[]{:S(2)}, u32[]{:S(2)}) async-start(bf16[8,112,1024]{2,1,0:T(8,128)(2,1)} %bitcast.128), calls=%async_computation.2 | async-start | bytes 3670016 | tf_op jit(solution)/shard_map/all_to_all | solution.py:167
  345.1 6.9 %psum.7 = f32[896]{0:T(1024)S(1)} all-reduce(f32[896]{0:T(1024)S(1)} %fusion.30), channel_id=1, replica_groups=mesh['exp'=8,'head'=4] {'head'}, use_global_device_ids=true, to_apply=%region_14.15 | all-reduce | flops 896 | bytes 7168 | tf_op jit(solution)/shard_map/psum | solution.py:154
  352.0 9.2 %all-gather.5.cloned.1.call-done = bf16[896,2,768]{0,2,1:T(8,128)(2,1)} async-done(((bf16[896,2,192]{0,2,1:T(8,128)(2,1)}), bf16[896,2,768]{0,2,1:T(8,128)(2,1)}) %all-gather.5.cloned.1.call-update) | async-done | bytes 2752528 | tf_op jit(solution)/shard_map/all_gather | solution.py:152
  361.2 7.2 %fusion.19 = bf16[896,1024]{1,0:T(8,128)(2,1)} fusion(bf16[896,1024]{1,0:T(8,128)(2,1)} %bitcast.120, bf16[896,2,768]{0,2,1:T(8,128)(2,1)} %all-gather.5.cloned.1.call-done, bf16[1024,2,768]{2,1,0:T(2,128)(2,1)S(1)} %bitcast.117, f32[896]{0:T(1024)S(1)} %psum.7, f32[896]{0:T(1024)S(1)} %multiply_multiply_fusion, f32[896]{0:T(1024)S(1)} %rsqrt_reduce_fusion), kind=kOutput, calls=%fused_computation.38 | convolution fusion | flops 2824077312 | bytes 9579008 | tf_op jit(solution)/shard_map/rkf,dkf->rd/dot_general | solution.py:158
  368.4 18.3 %all-to-all-done.1 = bf16[8,112,1024]{2,1,0:T(8,128)(2,1)} async-done(((bf16[8,112,1024]{2,1,0:T(8,128)(2,1)}), bf16[8,112,1024]{2,1,0:T(8,128)(2,1)}, u32[]{:S(2)}, u32[]{:S(2)}) %all-to-all-start.1) | async-done | bytes 1835040 | tf_op jit(solution)/shard_map/all_to_all | solution.py:167
  386.7 4.4 all-to-all-start.3
  392.3 6.3 %gather_fusion = bf16[768,1024]{1,0:T(8,128)(2,1)} fusion(bf16[896,1024]{1,0:T(8,128)(2,1)} %bitcast.13, s32[1024]{0:T(1024)S(1)} %pad_clamp_fusion), kind=kCustom, calls=%fused_computation | custom fusion | bytes 3148800 | tf_op jit(solution)/shard_map/gather | solution.py:170
  398.6 3.9 reshape.314
  402.5 30.9 %all-to-all-done.3 = bf16[8,112,1024]{2,1,0:T(8,128)(2,1)} async-done(((bf16[8,112,1024]{2,1,0:T(8,128)(2,1)}), bf16[8,112,1024]{2,1,0:T(8,128)(2,1)}, u32[]{:S(2)}, u32[]{:S(2)}) %all-to-all-start.3) | async-done | bytes 1835040 | tf_op jit(solution)/shard_map/all_to_all | solution.py:168
  433.4 6.3 %gather_fusion.1 = bf16[768,1024]{1,0:T(8,128)(2,1)} fusion(bf16[896,1024]{1,0:T(8,128)(2,1)} %bitcast.19, s32[1024]{0:T(1024)S(1)} %pad_clamp_fusion), kind=kCustom, calls=%fused_computation.1 | custom fusion | bytes 3148800 | tf_op jit(solution)/shard_map/gather | solution.py:173
  439.7 3.9 reshape.315
  443.6 6.6 %multiply_reduce_fusion = (f32[128,1024]{1,0:T(8,128)S(1)}, f32[128,1024]{1,0:T(8,128)S(1)}) fusion(f32[128,6,1024]{2,1,0:T(8,128)} %reshape.315, f32[128,6]{1,0:T(8,128)S(1)} %copy.70, f32[128,6,1024]{2,1,0:T(8,128)} %reshape.314), kind=kLoop, calls=%fused_computation.34 | loop fusion | flops 2883584 | bytes 7343104 | tf_op jit(solution)/shard_map/reduce_sum | solution.py:179
  (162 shorter events, 101.9 us)
Async XLA Ops:
  7.2 209.2 %copy-start = (bf16[1,1024,2,768]{3,2,1,0:T(2,128)(2,1)S(1)}, bf16[1,1024,2,768]{3,2,1,0:T(2,128)(2,1)}, u32[]{:S(2)}) copy-start(bf16[1,1024,2,768]{3,2,1,0:T(2,128)(2,1)} %param.13) | copy-start | bytes 9437188
  7.2 277.9 %reduce-scatter.4.cloned.1.call-start = ((), (), s32[]{:S(2)}) async-start(), calls=%async_computation.6 | async-start | bytes 6881280 | tf_op jit(solution)/shard_map/reduce_scatter | solution.py:135
  11.3 0.6 copy-start.9
  178.5 37.9 %copy-start.3 = (bf16[128,8,128]{0,2,1:T(8,128)(2,1)}, bf16[128,8,128]{0,2,1:T(8,128)(2,1)S(1)}, u32[]{:S(2)}) copy-start(bf16[128,8,128]{0,2,1:T(8,128)(2,1)S(1)} %divide_convert_fusion) | copy-start | bytes 786436
  216.4 1.3 copy-start.1
  223.0 0.9 copy-start.5
  223.0 90.2 %reduce-scatter.6.cloned.1.call-start = ((), (), s32[]{:S(2)}) async-start(), calls=%async_computation.8 | async-start | bytes 3440640 | tf_op jit(solution)/shard_map/reduce_scatter | solution.py:136
  225.6 42.0 %copy-start.12 = (bf16[1,768,1024]{2,1,0:T(8,128)(2,1)S(1)}, bf16[1,768,1024]{2,1,0:T(8,128)(2,1)}, u32[]{:S(2)}) copy-start(bf16[1,768,1024]{2,1,0:T(8,128)(2,1)} %param.14) | copy-start | bytes 4718596
  270.9 0.7 copy-start.13
  271.0 62.4 %all-gather.3.cloned.1.call-start = ((), (), s32[]{:S(2)}) async-start(), calls=%async_computation.7 | async-start | bytes 1720320 | tf_op jit(solution)/shard_map/all_gather | solution.py:151
  287.9 73.3 %all-gather.5.cloned.1.call-start = ((), (), s32[]{:S(2)}) async-start(), calls=%async_computation.9 | async-start | bytes 3440640 | tf_op jit(solution)/shard_map/all_gather | solution.py:152
  315.1 0.7 copy-start.2
  338.0 48.6 %all-to-all-start.1 = ((bf16[8,112,1024]{2,1,0:T(8,128)(2,1)}), bf16[8,112,1024]{2,1,0:T(8,128)(2,1)}, u32[]{:S(2)}, u32[]{:S(2)}) async-start(bf16[8,112,1024]{2,1,0:T(8,128)(2,1)} %bitcast.128), calls=%async_computation.2 | async-start | bytes 3670016 | tf_op jit(solution)/shard_map/all_to_all | solution.py:167
  386.7 4.5 copy-start.4
  386.7 5.3 %copy-start.8 = (s32[128,6]{1,0:T(8,128)S(1)}, s32[128,6]{1,0:T(8,128)}, u32[]{:S(2)}) copy-start(s32[128,6]{1,0:T(8,128)} %get-tuple-element.154) | copy-start | bytes 9220
  386.7 5.5 %copy-start.11 = (f32[128,6]{0,1:T(8,128)S(1)}, f32[128,6]{0,1:T(8,128)}, u32[]{:S(2)}) copy-start(f32[128,6]{0,1:T(8,128)} %param.16) | copy-start | bytes 9220
  386.7 5.6 %copy-start.10 = (s32[768]{0:T(1024)S(1)}, s32[768]{0:T(1024)}, u32[]{:S(2)}) copy-start(s32[768]{0:T(1024)} %copy-done.9) | copy-start | bytes 9220
  386.7 46.7 %all-to-all-start.3 = ((bf16[8,112,1024]{2,1,0:T(8,128)(2,1)}), bf16[8,112,1024]{2,1,0:T(8,128)(2,1)}, u32[]{:S(2)}, u32[]{:S(2)}) async-start(bf16[8,112,1024]{2,1,0:T(8,128)(2,1)} %bitcast.127), calls=%async_computation.5 | async-start | bytes 3670016 | tf_op jit(solution)/shard_map/all_to_all | solution.py:168
  443.6 6.6 %copy-start.6 = (bf16[128,1024]{1,0:T(8,128)(2,1)S(1)}, bf16[128,1024]{1,0:T(8,128)(2,1)}, u32[]{:S(2)}) copy-start(bf16[128,1024]{1,0:T(8,128)(2,1)} %param.17) | copy-start | bytes 786436
  443.6 6.6 %copy-start.7 = (bf16[128,1024]{1,0:T(8,128)(2,1)S(1)}, bf16[128,1024]{1,0:T(8,128)(2,1)}, u32[]{:S(2)}) copy-start(bf16[128,1024]{1,0:T(8,128)(2,1)} %copy.84) | copy-start | bytes 786436
Sparse Core Ops, SparseCore 0:
  223.2 52.0 reduce-scatter.3
  277.9 35.3 reduce-scatter.5
  314.8 18.5 all-gather.2
  334.8 26.3 all-gather.4
where the time goes:
time: 460 us; the launch traced here: 458 us
  blocking collectives  164 us (36%)
  waiting for transfers between devices  100 us (22%)
  other arithmetic  64.5 us (14%)
  matrix products  56 us (12%)
  local copies, waits for them, and re-layouts  48.3 us (10%)
  between operations  14 us (3%)
  starting transfers between devices  10.1 us (2%)
    all_to_all x1, blocking collectives, per_device(): lax.all_to_all(send_grads, 'exp', split_axis=0, concat_axis=0, tiled=True)  42 us
    all_to_all x1, blocking collectives, per_device(): lax.all_to_all(send_rows, 'exp', split_axis=0, concat_axis=0, tiled=True)  36.1 us
    all_gather x1, blocking collectives, per_device(): key_piece = lax.all_gather(keys, 'exp', axis=0, tiled=True)  35.4 us
    all_gather x1, blocking collectives, per_device(): value_piece = lax.all_gather(values, 'exp', axis=0, tiled=True)  33.6 us
    all_to_all x1, waiting for transfers between devices, per_device(): lax.all_to_all(expert_grad, 'exp', split_axis=0, concat_axis=0, tiled=True)  30.9 us
    reduce_scatter x1, waiting for transfers between devices, per_device(): lax.psum_scatter(back_sums[:, None, :], 'head', scatter_dimension=2, tile...  25.3 us
    all_to_all x1, waiting for transfers between devices, per_device(): lax.all_to_all(expert_out, 'exp', split_axis=0, concat_axis=0, tiled=True)  18.3 us
    dot_general x8, matrix products, block_partial(): jnp.einsum('btgij,bjgd->btgid', weights.astype(jnp.bfloat16), value_heads...  16.9 us
  transfers between devices with their start and end apart: 6, of which 5 were waited for; matrix products, arithmetic and copies ran while one was open for 8% of the time, Pallas kernels for 0%

commit v1 on v0

--- a/solution.py
+++ b/solution.py
@@ -1,6 +1,8 @@
 import jax
 import jax.numpy as jnp
 from jax import lax
+from jax.experimental import pallas as pl
+from jax.experimental.pallas import tpu as pltpu
 from jax.sharding import PartitionSpec as P
 
 D = 4096
@@ -182,7 +184,158 @@
     return (output.astype(jnp.bfloat16), grad_attended.astype(jnp.bfloat16))
 
 
+def attention_kernel(head_count, group, start_ref, q_ref, k_ref, v_ref, o_ref):
+    rows = q_ref.shape[0]
+    cached = k_ref.shape[0]
+    first = start_ref[0]
+    row_pos = first + lax.broadcasted_iota(jnp.int32, (rows, cached), 0)
+    visible = lax.broadcasted_iota(jnp.int32, (rows, cached), 1) <= row_pos
+    for head in range(head_count):
+        cols = slice(head * HEAD_WIDTH, (head + 1) * HEAD_WIDTH)
+        kv_head = head // group
+        kv_cols = slice(kv_head * HEAD_WIDTH, (kv_head + 1) * HEAD_WIDTH)
+        scores = lax.dot_general(
+            q_ref[:, cols],
+            k_ref[:, kv_cols],
+            (((1,), (1,)), ((), ())),
+            preferred_element_type=jnp.float32,
+        ) * HEAD_WIDTH ** (-0.5)
+        scores = jnp.where(visible, scores, hidden_logits)
+        best = jnp.max(scores, axis=1, keepdims=True)
+        weights = jnp.exp(scores - best)
+        total = jnp.sum(weights, axis=1, keepdims=True)
+        sums = jnp.dot(
+            weights.astype(jnp.bfloat16), v_ref[:, kv_cols], preferred_element_type=jnp.float32
+        )
+        o_ref[:, cols] = (sums / total).astype(jnp.bfloat16)
+
+
+def attend_local(queries, key_all, value_all, start):
+    head_count = queries.shape[1] // HEAD_WIDTH
+    group = head_count // (key_all.shape[1] // HEAD_WIDTH)
+
+    def body(*refs):
+        attention_kernel(head_count, group, *refs)
+
+    return pl.pallas_call(
+        body,
+        out_shape=jax.ShapeDtypeStruct(queries.shape, jnp.bfloat16),
+        in_specs=[pl.BlockSpec(memory_space=pltpu.SMEM)]
+        + [pl.BlockSpec(memory_space=pltpu.VMEM)] * 3,
+        out_specs=pl.BlockSpec(memory_space=pltpu.VMEM),
+        name="attention",
+    )(start.reshape(1).astype(jnp.int32), queries, key_all, value_all)
+
+
+def three_parts(value):
+    high = value.astype(jnp.bfloat16)
+    rest = value - high.astype(jnp.float32)
+    middle = rest.astype(jnp.bfloat16)
+    low = (rest - middle.astype(jnp.float32)).astype(jnp.bfloat16)
+    return high, middle, low
+
+
+def gather_exp(block, tag):
+    return lax.all_gather(block, "exp", axis=0, tiled=True)
+
+
+def dense_device(queries, keys, values, w_in, w_out, routes, route_weights, grad_out):
+    exp_count = lax.axis_size("exp")
+    exp_index = lax.axis_index("exp")
+    parts = lax.axis_size("head")
+    tokens, width = queries.shape
+    experts = w_in.shape[0] * exp_count
+    hidden = w_in.shape[3]
+    share = hidden // parts
+    kv_width = keys.shape[1]
+    offset = keys.shape[0] * exp_count - tokens * exp_count
+    w_first = w_in[0]
+    w_second = w_out[0]
+    kv_all = gather_exp(jnp.concatenate([keys, values], axis=1), 0)
+    hits = routes[:, :, None] == jnp.arange(experts, dtype=jnp.int32)[None, None, :]
+    table = jnp.sum(jnp.where(hits, route_weights[:, :, None], 0.0), axis=1)
+    packed = jnp.concatenate(three_parts(table), axis=1)
+    packed = jnp.pad(packed, ((0, 0), (0, -packed.shape[1] % 128)))
+    grad_pack = gather_exp(jnp.concatenate([grad_out, packed], axis=1), 1)
+    grads = grad_pack[:, :width]
+    attended = attend_local(
+        queries, kv_all[:, :kv_width], kv_all[:, kv_width:], offset + exp_index * tokens
+    )
+    rows = gather_exp(attended, 2)
+    count = rows.shape[0]
+    pieces = grad_pack[:, width : width + 3 * experts].astype(jnp.float32)
+    table_all = jnp.sum(pieces.reshape(count, 3, experts), axis=1)
+    own = (jnp.arange(experts) == exp_index).astype(jnp.float32)
+    gain = jnp.sum(table_all * own[None, :], axis=1)[:, None]
+    w_split = w_first.reshape(width, 2, parts, share)
+    second_split = w_second.reshape(parts, share, width)
+    back_sums = jnp.einsum(
+        "rd,hfd->hrf", grads, second_split, preferred_element_type=jnp.float32
+    ).astype(jnp.bfloat16)
+    back_value = lax.psum_scatter(back_sums, "head", scatter_dimension=0, tiled=False)
+    row_float = rows.astype(jnp.float32)
+    raw_sums = jnp.einsum("rd,dkhf->hrkf", rows, w_split, preferred_element_type=jnp.float32)
+    raw_sums = raw_sums.astype(jnp.bfloat16).reshape(parts, count, 2 * share)
+    squares = jnp.sum(row_float * row_float, axis=1)
+    square_tile = jnp.broadcast_to(
+        squares.astype(jnp.bfloat16)[None, :, None], (parts, count, 128)
+    )
+    raw_part = lax.psum_scatter(
+        jnp.concatenate([raw_sums, square_tile], axis=2),
+        "head",
+        scatter_dimension=0,
+        tiled=False,
+    ).astype(jnp.float32)
+    norm_scale = lax.rsqrt(raw_part[:, 2 * share : 2 * share + 1] / D + norm_eps)
+    gate_value = raw_part[:, :share] * norm_scale
+    up_value = raw_part[:, share : 2 * share] * norm_scale
+    back_value = back_value.astype(jnp.float32)
+    sigmoid = jax.nn.sigmoid(gate_value)
+    silu = gate_value * sigmoid
+    act = (silu * up_value).astype(jnp.bfloat16)
+    grad_gate = (back_value * up_value * sigmoid * (1.0 + gate_value * (1.0 - sigmoid))).astype(
+        jnp.bfloat16
+    )
+    grad_up = (back_value * silu).astype(jnp.bfloat16)
+    inner = jnp.sum(
+        grad_gate.astype(jnp.float32) * gate_value + grad_up.astype(jnp.float32) * up_value,
+        axis=1,
+        keepdims=True,
+    )
+    sent = jnp.concatenate([act, grad_gate, grad_up, *three_parts(inner)], axis=1)
+    sent = jnp.pad(sent, ((0, 0), (0, -sent.shape[1] % 128)))
+    whole = lax.all_gather(sent, "head", axis=0, tiled=False)
+    inner_sum = jnp.sum(whole[:, :, 3 * share : 3 * share + 3].astype(jnp.float32), axis=(0, 2))[
+        :, None
+    ]
+    act_all = jnp.transpose(whole[:, :, :share], (1, 0, 2)).reshape(count, hidden)
+    gate_all = jnp.transpose(whole[:, :, share : 2 * share], (1, 0, 2)).reshape(count, hidden)
+    up_all = jnp.transpose(whole[:, :, 2 * share : 3 * share], (1, 0, 2)).reshape(count, hidden)
+    grad_all = jnp.concatenate([gate_all, up_all], axis=1)
+    out_rows = jnp.dot(act_all, w_second, preferred_element_type=jnp.float32)
+    grad_normed = lax.dot_general(
+        grad_all,
+        w_first.reshape(width, 2 * hidden),
+        (((1,), (1,)), ((), ())),
+        preferred_element_type=jnp.float32,
+    )
+    grad_rows = norm_scale * grad_normed - row_float * (norm_scale * norm_scale / D) * inner_sum
+    routed = gain > 0.0
+    both = jnp.concatenate(
+        [
+            jnp.where(routed, gain * out_rows, 0.0).astype(jnp.bfloat16),
+            jnp.where(routed, gain * grad_rows, 0.0).astype(jnp.bfloat16),
+        ],
+        axis=1,
+    )
+    summed = lax.psum_scatter(both, "exp", scatter_dimension=0, tiled=True).astype(jnp.float32)
+    output = attended.astype(jnp.float32) + summed[:, :width]
+    grad_attended = grad_out.astype(jnp.float32) + summed[:, width:]
+    return (output.astype(jnp.bfloat16), grad_attended.astype(jnp.bfloat16))
+
+
 def solution(mesh):
+    dense = 2 * TOP >= mesh.shape["exp"]
     in_specs = (
         P("exp", "head"),
         P("exp", "head"),
@@ -195,5 +348,5 @@
     )
     out_specs = (P("exp", "head"), P("exp", "head"))
     return jax.shard_map(
-        per_device, mesh=mesh, in_specs=in_specs, out_specs=out_specs, check_vma=False
-    )
+        dense_device if dense else per_device, mesh=mesh, in_specs=in_specs, out_specs=out_specs, check_vma=False
+    )

time: 460 us -> 411 us (0.89)
  waiting for transfers between devices: 100 us -> 317 us
  blocking collectives: 164 us -> 0 us
  other arithmetic: 64.5 us -> 18 us
  matrix products: 56 us -> 17.6 us
  local copies, waits for them, and re-layouts: 48.3 us -> 37.9 us
  starting transfers between devices: 10.1 us -> 0.47 us
  Pallas kernels: 0 us -> 4.95 us
    all_gather x2 -> x4, waiting for transfers between devices: 25.8 us -> 161 us  [the longest x3 126 us: gather_exp(): return lax.all_gather(block, 'exp', axis=0, tiled=True)]
    reduce_scatter x2 -> x3, waiting for transfers between devices: 25.3 us -> 156 us  [the longest x1 88.4 us: dense_device(): lax.psum_scatter(both, 'exp', scatter_dimension=0, tiled=True)]
    all_to_all x2 -> x0, blocking collectives: 78.2 us -> none  [the longest x1 42 us: per_device(): lax.all_to_all(send_grads, 'exp', split_axis=0, concat_axis=0, tiled=True)]
    all_gather x2 -> x0, blocking collectives: 69 us -> none  [the longest x1 35.4 us: per_device(): key_piece = lax.all_gather(keys, 'exp', axis=0, tiled=True)]
    all_to_all x2 -> x0, waiting for transfers between devices: 49.2 us -> none  [the longest x1 30.9 us: per_device(): lax.all_to_all(expert_grad, 'exp', split_axis=0, concat_axis=0, tiled=True)]
    dot_general x22 -> x3, matrix products: 56 us -> 11.5 us  [the longest x1 5.06 us: dense_device(): lax.dot_general(grad_all, w_first.reshape(width, 2 * hidden), (((1,), (1,...]
    add x24 -> x0, other arithmetic: 27.1 us -> none  [the longest x8 16.6 us: fold_partials(): sums_now * old_factor[..., None]]
    reduce_sum x13 -> x6, other arithmetic: 20.5 us -> 4.95 us  [the longest x1 2.81 us: dense_device(): jnp.sum(grad_gate.astype(jnp.float32) * gate_value + grad_up.astype(jnp.f...]
  transfers between devices with their start and end apart: 6 -> 7, of which waited for: 5 -> 7; matrix products, arithmetic and copies ran while one was open for 8% -> 8% of each run, Pallas kernels for 0% -> 0%
where the time goes in v1:
time: 411 us; the launch traced here: 410 us
  waiting for transfers between devices  317 us (77%)
  local copies, waits for them, and re-layouts  37.9 us (9%)
  other arithmetic  18 us (4%)
  matrix products  17.6 us (4%)
  between operations  14.4 us (4%)
  Pallas kernels  4.95 us (1%)
    all_gather x3, waiting for transfers between devices, gather_exp(): return lax.all_gather(block, 'exp', axis=0, tiled=True)  126 us
    reduce_scatter x1, waiting for transfers between devices, dense_device(): lax.psum_scatter(both, 'exp', scatter_dimension=0, tiled=True)  88.4 us
    reduce_scatter x1, waiting for transfers between devices, dense_device(): lax.psum_scatter(jnp.concatenate([raw_sums, square_tile], axis=2), 'head'...  40.5 us
    all_gather x1, waiting for transfers between devices, dense_device(): whole = lax.all_gather(sent, 'head', axis=0, tiled=False)  35.1 us
    reduce_scatter x1, waiting for transfers between devices, dense_device(): lax.psum_scatter(back_sums, 'head', scatter_dimension=0, tiled=False)  27.1 us
    unnamed x32, local copies, waits for them, and re-layouts  17.9 us
    all_gather x1, local copies, waits for them, and re-layouts, dense_device(): whole = lax.all_gather(sent, 'head', axis=0, tiled=False)  9.54 us
  transfers between devices with their start and end apart: 7, of which 7 were waited for; matrix products, arithmetic and copies ran while one was open for 8% of the time, Pallas kernels for 0%

profile of v1, /device:TPU:0, one launch (start us, length us, event | category | flops | bytes accessed | tf_op | source)
XLA Modules:
  0.0 410.2 jit_solution(17576068550348092435)
XLA Ops:
  7.3 1.7 pad_maximum_fusion.3
  9.0 44.8 %all-gather.6.cloned.1.call-done = bf16[1024,512]{1,0:T(8,128)(2,1)} async-done(((bf16[128,512]{1,0:T(8,128)(2,1)}), bf16[1024,512]{1,0:T(8,128)(2,1)}) %all-gather.6.cloned.1.call-update) | async-done | bytes 1048592 | tf_op jit(solution)/shard_map/all_gather | solution.py:239
  53.7 2.3 fusion.37
  56.0 5.0 %attention.1 = bf16[128,1024]{1,0:T(8,128)(2,1)} custom-call(s32[1]{0:T(128)} %bitcast.refs_0_, bf16[128,1024]{1,0:T(8,128)(2,1)} %refs_1_.1, bf16[1024,256]{1,0:T(8,128)(2,1)} %get-tuple-element.14.refs_2_, bf16[1024,256]{1,0:T(8,128)(2,1)} %get-tuple-element.13.refs_3_), custom_call_target="tpu_custom_call" | custom-call | tf_op jit(solution)/shard_map/attention/pallas_call | solution.py:220
  61.3 0.7 pad_maximum_fusion.2
  62.1 8.7 %copy.46 = bf16[1,1024,2,768]{1,3,2,0:T(8,128)(2,1)} copy(bf16[1,1024,2,768]{3,2,1,0:T(2,128)(2,1)} %param.11) | data formatting | bytes 6291456 | tf_op args[3]
  70.8 38.1 %all-gather.10.cloned.1.call-done = bf16[1024,1024]{1,0:T(8,128)(2,1)} async-done(((bf16[128,1024]{1,0:T(8,128)(2,1)}), bf16[1024,1024]{1,0:T(8,128)(2,1)}) %all-gather.10.cloned.1.call-update) | async-done | bytes 2097168 | tf_op jit(solution)/shard_map/all_gather | solution.py:239
  108.9 6.0 %fusion.39 = f32[1024,1536]{0,1:S(1)} fusion(bf16[1024,1024]{1,0:T(8,128)(2,1)} %all-gather.10.cloned.1.call-done, bf16[1024,1536]{0,1:T(8,128)(2,1)} %bitcast.62), kind=kOutput, calls=%fused_computation.68 | convolution fusion | flops 3221225472 | bytes 11534336
  115.8 1.3 copy-done.4
  117.7 2.4 pad_maximum_fusion
  120.2 42.9 %all-gather.8.cloned.1.call-done = bf16[1024,1152]{0,1:T(8,128)(2,1)} async-done(((bf16[128,1152]{0,1:T(8,128)(2,1)}), bf16[1024,1152]{0,1:T(8,128)(2,1)}) %all-gather.8.cloned.1.call-update) | async-done | bytes 2359312 | tf_op jit(solution)/shard_map/all_gather | solution.py:239
  163.1 4.6 %fusion.15 = bf16[4,1024,192]{1,2,0:T(8,128)(2,1)} fusion(bf16[4,192,1024]{2,1,0:T(8,128)(2,1)S(1)} %bitcast.57, bf16[1024,1152]{0,1:T(8,128)(2,1)} %all-gather.8.cloned.1.call-done), kind=kOutput, calls=%fused_computation.20 | convolution fusion | flops 1611399168 | bytes 5242880 | tf_op jit(solution)/shard_map/rd,hfd->hrf/dot_general | solution.py:272
  167.8 40.5 %reduce-scatter.4.cloned.1.call-done = bf16[1,1024,512]{1,2,0:T(8,128)(2,1)} async-done(((bf16[4,1024,512]{1,2,0:T(8,128)(2,1)}), bf16[1,1024,512]{1,2,0:T(8,128)(2,1)}) %reduce-scatter.4.cloned.1.call-update) | async-done | bytes 1048592 | tf_op jit(solution)/shard_map/reduce_scatter | solution.py:283
  208.2 1.5 bitcast_convert_fusion
  209.7 1.3 copy-done.1
  211.7 27.1 %reduce-scatter.6.cloned.1.call-done = bf16[1,1024,192]{1,2,0:T(8,128)(2,1)} async-done(((bf16[4,1024,192]{1,2,0:T(8,128)(2,1)}), bf16[1,1024,192]{1,2,0:T(8,128)(2,1)}) %reduce-scatter.6.cloned.1.call-update) | async-done | bytes 393232 | tf_op jit(solution)/shard_map/reduce_scatter | solution.py:275
  238.7 2.8 add_reduce_fusion
  242.7 2.8 concatenate.25
  245.6 1.3 pad.9
  247.1 4.3 %copy.61 = bf16[128,8,2,768]{3,1,2,0:T(8,128)(2,1)} copy(bf16[128,8,2,768]{3,2,1,0:T(2,128)(2,1)} %bitcast.58) | data formatting | bytes 6291456
  251.3 0.8 convert_reduce_fusion
  252.3 35.1 %all-gather.12.cloned.1.call-done = bf16[4096,640]{0,1:T(8,128)(2,1)} async-done(((bf16[1024,640]{0,1:T(8,128)(2,1)}), bf16[4096,640]{0,1:T(8,128)(2,1)}) %all-gather.12.cloned.1.call-update) | async-done | bytes 5242896 | tf_op jit(solution)/shard_map/all_gather | solution.py:307
  287.4 9.5 %reshape.96 = bf16[4,1024,640]{1,0,2:T(4,128)(2,1)} reshape(bf16[4096,640]{0,1:T(8,128)(2,1)} %all-gather.12.cloned.1.call-done) | data formatting | bytes 10485760 | tf_op jit(solution)/shard_map/all_gather | solution.py:307
  296.9 3.7 fusion.36
  300.6 0.8 convert_reduce_fusion.1
  302.9 1.9 select_convert_fusion
  304.7 0.6 copy-done.5
  305.4 5.1 %fusion.5 = bf16[1024,1024]{1,0:T(8,128)(2,1)S(1)} fusion(bf16[1024,1024]{1,0:T(8,128)(2,1)S(1)} %copy-done.5, bf16[1024,1536]{1,0:T(8,128)(2,1)S(1)} %bitcast.61, bf16[1024,768]{0,1:T(8,128)(2,1)S(1)} %bitcast.64, bf16[1024,768]{0,1:T(8,128)(2,1)S(1)} %bitcast.63, f32[1024]{0:T(1024)S(1)} %convert_reduce_fusion.1, f32[1024]{0:T(1024)S(1)} %bitcast.70, ...), kind=kOutput, calls=%fused_computation.7 | convolution fusion | flops 3235905536 | bytes 10503168 | tf_op jit(solution)/shard_map/dot_general | solution.py:316
  310.4 2.4 pad_maximum_fusion.1
  312.9 88.4 %reduce-scatter.8.cloned.1.call-done = bf16[128,2048]{1,0:T(8,128)(2,1)} async-done(((bf16[1024,2048]{1,0:T(8,128)(2,1)}), bf16[128,2048]{1,0:T(8,128)(2,1)}) %reduce-scatter.8.cloned.1.call-update) | async-done | bytes 524304 | tf_op jit(solution)/shard_map/reduce_scatter | solution.py:331
  401.3 1.1 convert_element_type.201
  402.5 0.9 fusion.21
  (54 shorter events, 5.5 us)
Async XLA Ops:
  7.2 155.9 %copy-start = (bf16[1,768,1024]{2,1,0:T(8,128)(2,1)S(1)}, bf16[1,768,1024]{2,1,0:T(8,128)(2,1)}, u32[]{:S(2)}) copy-start(bf16[1,768,1024]{2,1,0:T(8,128)(2,1)} %param.12) | copy-start | bytes 4718596
  7.2 53.9 %copy-start.6 = (bf16[128,1024]{1,0:T(8,128)(2,1)S(1)}, bf16[128,1024]{1,0:T(8,128)(2,1)}, u32[]{:S(2)}) copy-start(bf16[128,1024]{1,0:T(8,128)(2,1)} %param.15) | copy-start | bytes 786436
  7.2 54.0 %copy-start.11 = (s32[128,6]{0,1:T(8,128)S(1)}, s32[128,6]{0,1:T(8,128)}, u32[]{:S(2)}) copy-start(s32[128,6]{0,1:T(8,128)} %param.13) | copy-start | bytes 9220
  7.2 54.0 %copy-start.10 = (f32[128,6]{0,1:T(8,128)S(1)}, f32[128,6]{0,1:T(8,128)}, u32[]{:S(2)}) copy-start(f32[128,6]{0,1:T(8,128)} %param.14) | copy-start | bytes 9220
  7.2 46.5 %all-gather.6.cloned.1.call-start = ((), (), s32[]{:S(2)}) async-start(), calls=%async_computation.3 | async-start | bytes 1179648 | tf_op jit(solution)/shard_map/all_gather | solution.py:239
  8.9 100.0 %all-gather.10.cloned.1.call-start = ((), (), s32[]{:S(2)}) async-start(), calls=%async_computation.5 | async-start | bytes 2359296 | tf_op jit(solution)/shard_map/all_gather | solution.py:239
  61.0 102.1 %all-gather.8.cloned.1.call-start = ((), (), s32[]{:S(2)}) async-start(), calls=%async_computation.4 | async-start | bytes 2654208 | tf_op jit(solution)/shard_map/all_gather | solution.py:239
  62.0 146.2 %reduce-scatter.4.cloned.1.call-start = ((), (), s32[]{:S(2)}) async-start(), calls=%async_computation.6 | async-start | bytes 5242880 | tf_op jit(solution)/shard_map/reduce_scatter | solution.py:283
  115.5 1.7 copy-start.4
  120.2 118.6 %reduce-scatter.6.cloned.1.call-start = ((), (), s32[]{:S(2)}) async-start(), calls=%async_computation.7 | async-start | bytes 1966080 | tf_op jit(solution)/shard_map/reduce_scatter | solution.py:275
  167.7 119.7 %all-gather.12.cloned.1.call-start = ((), (), s32[]{:S(2)}) async-start(), calls=%async_computation.9 | async-start | bytes 6553600 | tf_op jit(solution)/shard_map/all_gather | solution.py:307
  209.7 1.3 copy-start.1
  211.7 31.1 %copy-start.8 = (f32[1024,1]{0,1:T(1,128)}, f32[1024,1]{0,1:T(1,128)S(1)}, u32[]{:S(2)}) copy-start(f32[1024,1]{0,1:T(1,128)S(1)} %get-tuple-element.3) | copy-start | bytes 12292
  246.8 154.4 %reduce-scatter.8.cloned.1.call-start = ((), (), s32[]{:S(2)}) async-start(), calls=%async_computation.8 | async-start | bytes 4718592 | tf_op jit(solution)/shard_map/reduce_scatter | solution.py:331
  302.8 1.9 copy-start.2
  302.8 2.5 copy-start.5
  302.8 2.5 copy-start.9
  302.8 2.5 copy-start.12
  312.8 89.6 %copy-start.3 = (bf16[128,1024]{1,0:T(8,128)(2,1)S(1)}, bf16[128,1024]{1,0:T(8,128)(2,1)}, u32[]{:S(2)}) copy-start(bf16[128,1024]{1,0:T(8,128)(2,1)} %attention.1) | copy-start | bytes 786436
  312.8 89.6 %copy-start.7 = (bf16[128,1024]{1,0:T(8,128)(2,1)S(1)}, bf16[128,1024]{1,0:T(8,128)(2,1)}, u32[]{:S(2)}) copy-start(bf16[128,1024]{1,0:T(8,128)(2,1)} %param.15) | copy-start | bytes 786436
Sparse Core Ops, SparseCore 0:
  10.7 42.9 all-gather.5
  61.1 47.7 all-gather.9
  111.0 52.0 all-gather.7
  165.4 42.7 reduce-scatter.3
  210.6 28.0 reduce-scatter.5
  247.0 40.3 all-gather.11
  313.0 88.2 reduce-scatter.7

commit v2 on v1

--- a/solution.py
+++ b/solution.py
@@ -235,8 +235,157 @@
     return high, middle, low
 
 
+def ring_place(index, count):
+    outer, inner = index // 2, index % 2
+    return outer + inner * (count - 1 - 2 * outer)
+
+
+def ring_index(place, count):
+    inner = place // (count // 2)
+    return 2 * (place + inner * (count - 1 - 2 * place)) + inner
+
+
+def ring_start(count):
+    place = ring_place(lax.axis_index("exp"), count)
+    right = ring_index((place + 1) % count, count)
+    left = ring_index((place + count - 1) % count, count)
+    barrier = pltpu.get_barrier_semaphore()
+    for other in (left, right):
+        pl.semaphore_signal(
+            barrier, inc=1, device_id={"exp": other}, device_id_type=pl.DeviceIdType.MESH
+        )
+    pl.semaphore_wait(barrier, 2)
+    return place, (right, left)
+
+
+def ring_lanes(count):
+    reach = count // 2
+    return ((0, 0, reach), (1, 1, reach), (0, 1, reach - 1), (1, 0, reach - 1))
+
+
+def ring_gather(count, x_ref, out_ref, send_sem, recv_sem, own_sem):
+    place, others = ring_start(count)
+    me = lax.axis_index("exp")
+    rows = x_ref.shape[0]
+    half = rows // 2
+    own = pltpu.make_async_copy(
+        x_ref, out_ref.at[pl.ds(pl.multiple_of(me * rows, rows), rows)], own_sem
+    )
+    own.start()
+
+    def copy(way, part, step):
+        shift = count - step if way == 0 else step
+        owner = ring_index((place + shift) % count, count)
+        spot = out_ref.at[pl.ds(pl.multiple_of(owner * rows + part * half, half), half)]
+        source = x_ref.at[pl.ds(part * half, half)] if step == 0 else spot
+        return pltpu.make_async_remote_copy(
+            src_ref=source,
+            dst_ref=spot,
+            send_sem=send_sem.at[way, part, step],
+            recv_sem=recv_sem.at[way, part, step],
+            device_id={"exp": others[way]},
+            device_id_type=pl.DeviceIdType.MESH,
+        )
+
+    copies = {}
+    for step in range(count // 2):
+        for way, part, steps in ring_lanes(count):
+            if step < steps:
+                if step > 0:
+                    copies[way, part, step - 1].wait_recv()
+                copies[way, part, step] = copy(way, part, step)
+                copies[way, part, step].start()
+    for way, part, steps in ring_lanes(count):
+        copies[way, part, steps - 1].wait_recv()
+    for each in copies.values():
+        each.wait_send()
+    own.wait()
+
+
+def ring_scatter(count, x_ref, out_ref, held, send_sem, recv_sem):
+    place, others = ring_start(count)
+    rows = x_ref.shape[1]
+    half = rows // 2
+
+    def term(way, part, step, steps):
+        shift = steps - step if way == 0 else count - steps + step
+        return x_ref.at[ring_index((place + shift) % count, count), pl.ds(part * half, half)]
+
+    copies = {}
+    for step in range(count // 2):
+        for way, part, steps in ring_lanes(count):
+            if step < steps:
+                source = term(way, part, step, steps)
+                if step > 0:
+                    copies[way, part, step - 1].wait_recv()
+                    slot = held.at[way, step - 1, pl.ds(part * half, half)]
+                    slot[...] = (
+                        slot[...].astype(jnp.float32) + source[...].astype(jnp.float32)
+                    ).astype(jnp.bfloat16)
+                    source = slot
+                copies[way, part, step] = pltpu.make_async_remote_copy(
+                    src_ref=source,
+                    dst_ref=held.at[way, step, pl.ds(part * half, half)],
+                    send_sem=send_sem.at[way, part, step],
+                    recv_sem=recv_sem.at[way, part, step],
+                    device_id={"exp": others[way]},
+                    device_id_type=pl.DeviceIdType.MESH,
+                )
+                copies[way, part, step].start()
+    last = {}
+    for way, part, steps in ring_lanes(count):
+        copies[way, part, steps - 1].wait_recv()
+        last[way, part] = steps - 1
+    me = lax.axis_index("exp")
+    for part in range(2):
+        span = pl.ds(part * half, half)
+        out_ref[span] = (
+            x_ref[me, span].astype(jnp.float32)
+            + held[0, last[0, part], span].astype(jnp.float32)
+            + held[1, last[1, part], span].astype(jnp.float32)
+        )
+    for each in copies.values():
+        each.wait_send()
+
+
+def ring_sems(count):
+    return [pltpu.SemaphoreType.DMA((2, 2, count // 2))] * 2
+
+
 def gather_exp(block, tag):
-    return lax.all_gather(block, "exp", axis=0, tiled=True)
+    count = lax.axis_size("exp")
+    rows, width = block.shape
+
+    def gather_body(*refs):
+        ring_gather(count, *refs)
+
+    return pl.pallas_call(
+        gather_body,
+        out_shape=jax.ShapeDtypeStruct((count * rows, width), block.dtype),
+        in_specs=[pl.BlockSpec(memory_space=pltpu.VMEM)],
+        out_specs=pl.BlockSpec(memory_space=pltpu.VMEM),
+        scratch_shapes=ring_sems(count) + [pltpu.SemaphoreType.DMA],
+        compiler_params=pltpu.CompilerParams(collective_id=tag, has_side_effects=True),
+        name="ring_gather_" + str(tag),
+    )(block)
+
+
+def scatter_exp(blocks, tag):
+    count, rows, width = blocks.shape
+
+    def scatter_body(*refs):
+        ring_scatter(count, *refs)
+
+    return pl.pallas_call(
+        scatter_body,
+        out_shape=jax.ShapeDtypeStruct((rows, width), jnp.float32),
+        in_specs=[pl.BlockSpec(memory_space=pltpu.VMEM)],
+        out_specs=pl.BlockSpec(memory_space=pltpu.VMEM),
+        scratch_shapes=[pltpu.VMEM((2, count // 2, rows, width), blocks.dtype)]
+        + ring_sems(count),
+        compiler_params=pltpu.CompilerParams(collective_id=tag, has_side_effects=True),
+        name="ring_scatter",
+    )(blocks)
 
 
 def dense_device(queries, keys, values, w_in, w_out, routes, route_weights, grad_out):
@@ -251,12 +400,13 @@
     offset = keys.shape[0] * exp_count - tokens * exp_count
     w_first = w_in[0]
     w_second = w_out[0]
-    kv_all = gather_exp(jnp.concatenate([keys, values], axis=1), 0)
     hits = routes[:, :, None] == jnp.arange(experts, dtype=jnp.int32)[None, None, :]
     table = jnp.sum(jnp.where(hits, route_weights[:, :, None], 0.0), axis=1)
     packed = jnp.concatenate(three_parts(table), axis=1)
     packed = jnp.pad(packed, ((0, 0), (0, -packed.shape[1] % 128)))
-    grad_pack = gather_exp(jnp.concatenate([grad_out, packed], axis=1), 1)
+    early = gather_exp(jnp.concatenate([keys, values, grad_out, packed], axis=1), 1)
+    kv_all = early[:, : 2 * kv_width]
+    grad_pack = early[:, 2 * kv_width :]
     grads = grad_pack[:, :width]
     attended = attend_local(
         queries, kv_all[:, :kv_width], kv_all[:, kv_width:], offset + exp_index * tokens
@@ -328,14 +478,14 @@
         ],
         axis=1,
     )
-    summed = lax.psum_scatter(both, "exp", scatter_dimension=0, tiled=True).astype(jnp.float32)
+    summed = scatter_exp(both.reshape(exp_count, tokens, 2 * width), 3)
     output = attended.astype(jnp.float32) + summed[:, :width]
     grad_attended = grad_out.astype(jnp.float32) + summed[:, width:]
     return (output.astype(jnp.bfloat16), grad_attended.astype(jnp.bfloat16))
 
 
 def solution(mesh):
-    dense = 2 * TOP >= mesh.shape["exp"]
+    dense = 2 * TOP >= mesh.shape["exp"] and mesh.shape["exp"] % 2 == 0
     in_specs = (
         P("exp", "head"),
         P("exp", "head"),

time: 411 us -> 308 us (0.75)
  waiting for transfers between devices: 317 us -> 101 us
  Pallas kernels: 4.95 us -> 117 us
    all_gather x3 -> x0, waiting for transfers between devices: 126 us -> none  [gather_exp(): return lax.all_gather(block, 'exp', axis=0, tiled=True)]
    pallas_call x0 -> x3, Pallas kernels: none -> 112 us  [the longest x2 65.3 us: gather_exp(): pl.pallas_call(gather_body, out_shape=jax.ShapeDtypeStruct((count * rows,...]
    reduce_scatter x1 -> x0, waiting for transfers between devices: 88.4 us -> none  [dense_device(): lax.psum_scatter(both, 'exp', scatter_dimension=0, tiled=True)]
    unnamed x32 -> x23, local copies, waits for them, and re-layouts: 17.9 us -> 16.3 us
  transfers between devices with their start and end apart: 7 -> 3, of which waited for: 7 -> 3; matrix products, arithmetic and copies ran while one was open for 8% -> 4% of each run, Pallas kernels for 0% -> 0%
where the time goes in v2:
time: 308 us; the launch traced here: 307 us
  Pallas kernels  117 us (38%)
  waiting for transfers between devices  101 us (33%)
  local copies, waits for them, and re-layouts  36.6 us (12%)
  other arithmetic  20 us (6%)
  matrix products  17.5 us (6%)
  between operations  14 us (5%)
    pallas_call x2, Pallas kernels, gather_exp(): pl.pallas_call(gather_body, out_shape=jax.ShapeDtypeStruct((count * rows,...  65.3 us
    pallas_call x1, Pallas kernels, scatter_exp(): pl.pallas_call(scatter_body, out_shape=jax.ShapeDtypeStruct((rows, width)...  46.8 us
    reduce_scatter x1, waiting for transfers between devices, dense_device(): lax.psum_scatter(jnp.concatenate([raw_sums, square_tile], axis=2), 'head'...  38.9 us
    all_gather x1, waiting for transfers between devices, dense_device(): whole = lax.all_gather(sent, 'head', axis=0, tiled=False)  35.1 us
    reduce_scatter x1, waiting for transfers between devices, dense_device(): lax.psum_scatter(back_sums, 'head', scatter_dimension=0, tiled=False)  27.2 us
    unnamed x23, local copies, waits for them, and re-layouts  16.3 us
    all_gather x1, local copies, waits for them, and re-layouts, dense_device(): whole = lax.all_gather(sent, 'head', axis=0, tiled=False)  9.49 us
  transfers between devices with their start and end apart: 3, of which 3 were waited for; matrix products, arithmetic and copies ran while one was open for 4% of the time, Pallas kernels for 0%

profile of v2, /device:TPU:0, one launch (start us, length us, event | category | flops | bytes accessed | tf_op | source)
XLA Modules:
  0.0 306.5 jit_solution(12358835989191123621)
XLA Ops:
  7.2 0.8 select_reduce_fusion
  8.2 1.8 fusion.28.refs_0_
  9.9 40.3 %ring_gather_1.1 = bf16[1024,1664]{1,0:T(8,128)(2,1)} custom-call(bf16[128,1664]{1,0:T(8,128)(2,1)} %fusion.28.refs_0_), custom_call_target="tpu_custom_call" | custom-call | tf_op jit(solution)/shard_map/ring_gather_1/pallas_call | solution.py:362
  50.2 2.3 fusion.38
  52.5 5.0 %attention.1.refs_0_ = bf16[128,1024]{1,0:T(8,128)(2,1)} custom-call(s32[1]{0:T(128)} %bitcast.refs_0_, bf16[128,1024]{1,0:T(8,128)(2,1)} %refs_1_.1, bf16[1024,256]{1,0:T(8,128)(2,1)} %get-tuple-element.11.refs_2_, bf16[1024,256]{1,0:T(8,128)(2,1)} %get-tuple-element.10.refs_3_), custom_call_target="tpu_custom_call" | custom-call | tf_op jit(solution)/shard_map/attention/pallas_call | solution.py:220
  57.5 25.0 %ring_gather_2.1 = bf16[1024,1024]{1,0:T(8,128)(2,1)} custom-call(bf16[128,1024]{1,0:T(8,128)(2,1)} %attention.1.refs_0_), custom_call_target="tpu_custom_call" | custom-call | tf_op jit(solution)/shard_map/ring_gather_2/pallas_call | solution.py:362
  82.4 2.1 fusion
  84.5 8.7 %copy.47 = bf16[1,1024,2,768]{1,3,2,0:T(8,128)(2,1)} copy(bf16[1,1024,2,768]{3,2,1,0:T(2,128)(2,1)} %param.11) | data formatting | bytes 6291456 | tf_op args[3]
  93.2 6.0 %fusion.40 = f32[1024,1536]{0,1:S(1)} fusion(bf16[1024,1024]{1,0:T(8,128)(2,1)} %ring_gather_2.1, bf16[1024,1536]{0,1:T(8,128)(2,1)} %bitcast.61), kind=kOutput, calls=%fused_computation.63 | convolution fusion | flops 3221225472 | bytes 11534336
  100.1 2.4 pad_maximum_fusion
  102.6 4.6 %fusion.19 = bf16[4,1024,192]{1,2,0:T(8,128)(2,1)} fusion(bf16[4,192,1024]{2,1,0:T(8,128)(2,1)S(1)} %bitcast.55, bf16[1024,1664]{1,0:T(8,128)(2,1)} %ring_gather_1.1), kind=kOutput, calls=%fused_computation.21 | convolution fusion | flops 1611399168 | bytes 5242880 | tf_op jit(solution)/shard_map/rd,hfd->hrf/dot_general | solution.py:422
  107.4 38.9 %reduce-scatter.3.cloned.1.call-done = bf16[1,1024,512]{1,2,0:T(8,128)(2,1)} async-done(((bf16[4,1024,512]{1,2,0:T(8,128)(2,1)}), bf16[1,1024,512]{1,2,0:T(8,128)(2,1)}) %reduce-scatter.3.cloned.1.call-update) | async-done | bytes 1048592 | tf_op jit(solution)/shard_map/reduce_scatter | solution.py:433
  146.3 1.5 bitcast_convert_fusion
  147.8 1.4 copy-done.2
  149.2 0.6 multiply_multiply_fusion
  149.8 27.2 %reduce-scatter.5.cloned.1.call-done = bf16[1,1024,192]{1,2,0:T(8,128)(2,1)} async-done(((bf16[4,1024,192]{1,2,0:T(8,128)(2,1)}), bf16[1,1024,192]{1,2,0:T(8,128)(2,1)}) %reduce-scatter.5.cloned.1.call-update) | async-done | bytes 393232 | tf_op jit(solution)/shard_map/reduce_scatter | solution.py:425
  177.0 2.8 add_reduce_fusion
  180.4 0.6 subtract_convert_fusion
  181.0 2.8 concatenate.21
  183.8 1.3 pad.9
  185.1 1.0 slice_convert_fusion
  186.3 4.2 %copy.59 = bf16[128,8,2,768]{3,1,2,0:T(8,128)(2,1)} copy(bf16[128,8,2,768]{3,2,1,0:T(2,128)(2,1)} %bitcast.57) | data formatting | bytes 6291456
  190.6 35.1 %all-gather.3.cloned.1.call-done = bf16[4096,640]{0,1:T(8,128)(2,1)} async-done(((bf16[1024,640]{0,1:T(8,128)(2,1)}), bf16[4096,640]{0,1:T(8,128)(2,1)}) %all-gather.3.cloned.1.call-update) | async-done | bytes 5242896 | tf_op jit(solution)/shard_map/all_gather | solution.py:457
  225.7 9.5 %reshape.100 = bf16[4,1024,640]{1,0,2:T(4,128)(2,1)} reshape(bf16[4096,640]{0,1:T(8,128)(2,1)} %all-gather.3.cloned.1.call-done) | data formatting | bytes 10485760 | tf_op jit(solution)/shard_map/all_gather | solution.py:457
  235.2 0.8 convert_reduce_fusion
  235.9 3.7 %fusion.37 = (bf16[4,1024,192]{1,0,2:T(4,128)(2,1)S(1)}, bf16[4,1024,192]{1,0,2:T(4,128)(2,1)S(1)}, bf16[4,1024,192]{1,0,2:T(4,128)(2,1)S(1)}) fusion(bf16[4,1024,640]{1,0,2:T(4,128)(2,1)} %reshape.100), kind=kLoop, calls=%fused_computation.60 | loop fusion | bytes 9437184 | tf_op jit(solution)/shard_map/slice | solution.py:461
  241.1 1.9 select_convert_fusion
  243.0 0.6 copy-done.3
  243.6 5.1 %fusion.5 = bf16[1024,1024]{1,0:T(8,128)(2,1)S(1)} fusion(bf16[1024,1024]{1,0:T(8,128)(2,1)S(1)} %copy-done.1, bf16[1024,1536]{1,0:T(8,128)(2,1)S(1)} %bitcast.60, bf16[1024,768]{0,1:T(8,128)(2,1)S(1)} %bitcast.63, bf16[1024,768]{0,1:T(8,128)(2,1)S(1)} %bitcast.62, f32[1024]{0:T(1024)S(1)} %convert_reduce_fusion, f32[1024]{0:T(1024)S(1)} %bitcast.69, ...), kind=kOutput, calls=%fused_computation.7 | convolution fusion | flops 3235905536 | bytes 10503168 | tf_op jit(solution)/shard_map/dot_general | solution.py:466
  248.7 2.4 pad_maximum_fusion.1
  251.0 46.8 %ring_scatter.1 = f32[128,2048]{1,0:T(8,128)} custom-call(bf16[8,128,2048]{2,1,0:T(8,128)(2,1)} %bitcast.56), custom_call_target="tpu_custom_call" | custom-call | tf_op jit(solution)/shard_map/ring_scatter/pallas_call | solution.py:379
  297.9 2.1 add_convert_fusion
  (37 shorter events, 3.7 us)
Async XLA Ops:
  7.2 95.4 %copy-start = (bf16[1,768,1024]{2,1,0:T(8,128)(2,1)S(1)}, bf16[1,768,1024]{2,1,0:T(8,128)(2,1)}, u32[]{:S(2)}) copy-start(bf16[1,768,1024]{2,1,0:T(8,128)(2,1)} %param.12) | copy-start | bytes 4718596
  7.2 139.2 %reduce-scatter.3.cloned.1.call-start = ((), (), s32[]{:S(2)}) async-start(), calls=%async_computation.2 | async-start | bytes 5242880 | tf_op jit(solution)/shard_map/reduce_scatter | solution.py:433
  102.5 74.4 %reduce-scatter.5.cloned.1.call-start = ((), (), s32[]{:S(2)}) async-start(), calls=%async_computation.3 | async-start | bytes 1966080 | tf_op jit(solution)/shard_map/reduce_scatter | solution.py:425
  107.2 118.5 %all-gather.3.cloned.1.call-start = ((), (), s32[]{:S(2)}) async-start(), calls=%async_computation.4 | async-start | bytes 6553600 | tf_op jit(solution)/shard_map/all_gather | solution.py:457
  147.8 1.4 copy-start.2
  149.8 31.2 %copy-start.6 = (f32[1024,1]{0,1:T(1,128)}, f32[1024,1]{0,1:T(1,128)S(1)}, u32[]{:S(2)}) copy-start(f32[1024,1]{0,1:T(1,128)S(1)} %get-tuple-element.3) | copy-start | bytes 12292
  241.1 1.9 copy-start.1
  241.1 2.5 copy-start.3
  241.1 2.5 copy-start.7
  241.1 2.5 copy-start.8
  251.0 46.8 %copy-start.4 = (bf16[128,1024]{1,0:T(8,128)(2,1)S(1)}, bf16[128,1024]{1,0:T(8,128)(2,1)}, u32[]{:S(2)}) copy-start(bf16[128,1024]{1,0:T(8,128)(2,1)} %attention.1.refs_0_) | copy-start | bytes 786436
  251.0 46.8 %copy-start.5 = (bf16[128,1024]{1,0:T(8,128)(2,1)S(1)}, bf16[128,1024]{1,0:T(8,128)(2,1)}, u32[]{:S(2)}) copy-start(bf16[128,1024]{1,0:T(8,128)(2,1)} %param.15) | copy-start | bytes 786436
Sparse Core Ops, SparseCore 0:
  102.7 43.6 reduce-scatter.2
  148.9 28.0 reduce-scatter.4
  185.2 40.3 all-gather.2

commit v3 on v2

--- a/solution.py
+++ b/solution.py
@@ -388,6 +388,139 @@
     )(blocks)
 
 
+def pair_start():
+    me = lax.axis_index("head")
+    mate = me + 1 - 2 * (me % 2)
+    across = (me + 2) % 4
+    barrier = pltpu.get_barrier_semaphore()
+    for other in (mate, across):
+        pl.semaphore_signal(
+            barrier, inc=1, device_id={"head": other}, device_id_type=pl.DeviceIdType.MESH
+        )
+    pl.semaphore_wait(barrier, 2)
+    return me, mate, across
+
+
+def pair_copy(source, target, send_sem, recv_sem, other):
+    copy = pltpu.make_async_remote_copy(
+        src_ref=source,
+        dst_ref=target,
+        send_sem=send_sem,
+        recv_sem=recv_sem,
+        device_id={"head": other},
+        device_id_type=pl.DeviceIdType.MESH,
+    )
+    copy.start()
+    return copy
+
+
+def pair_scatter(chunks, x_ref, out_ref, near, far, send_sem, recv_sem):
+    me, mate, across = pair_start()
+    step = x_ref.shape[1] // chunks
+    spans = [pl.ds(part * step, step) for part in range(chunks)]
+    copies = {}
+    for kind, dest in ((0, (mate + 2) % 4), (1, mate)):
+        for part, span in enumerate(spans):
+            copies[kind, part] = pair_copy(
+                x_ref.at[dest, span],
+                near.at[kind, span],
+                send_sem.at[kind, part],
+                recv_sem.at[kind, part],
+                mate,
+            )
+    for part, span in enumerate(spans):
+        copies[0, part].wait_recv()
+        near[0, span] = (
+            near[0, span].astype(jnp.float32) + x_ref[across, span].astype(jnp.float32)
+        ).astype(jnp.bfloat16)
+        copies[2, part] = pair_copy(
+            near.at[0, span], far.at[span], send_sem.at[2, part], recv_sem.at[2, part], across
+        )
+    for part, span in enumerate(spans):
+        copies[1, part].wait_recv()
+        copies[2, part].wait_recv()
+        out_ref[span] = (
+            x_ref[me, span].astype(jnp.float32)
+            + near[1, span].astype(jnp.float32)
+            + far[span].astype(jnp.float32)
+        )
+    for each in copies.values():
+        each.wait_send()
+
+
+def pair_gather(chunks, x_ref, out_ref, send_sem, recv_sem, own_sem):
+    me, mate, across = pair_start()
+    own = pltpu.make_async_copy(x_ref, out_ref.at[me], own_sem)
+    own.start()
+    step = x_ref.shape[0] // chunks
+    spans = [pl.ds(part * step, step) for part in range(chunks)]
+    copies = {}
+    for kind, other in ((0, across), (1, mate)):
+        for part, span in enumerate(spans):
+            copies[kind, part] = pair_copy(
+                x_ref.at[span],
+                out_ref.at[me, span],
+                send_sem.at[kind, part],
+                recv_sem.at[kind, part],
+                other,
+            )
+    for part, span in enumerate(spans):
+        copies[0, part].wait_recv()
+        copies[2, part] = pair_copy(
+            out_ref.at[across, span],
+            out_ref.at[across, span],
+            send_sem.at[2, part],
+            recv_sem.at[2, part],
+            mate,
+        )
+    for part in range(chunks):
+        copies[1, part].wait_recv()
+        copies[2, part].wait_recv()
+    for each in copies.values():
+        each.wait_send()
+    own.wait()
+
+
+def pair_sems(chunks):
+    return [pltpu.SemaphoreType.DMA((3, chunks))] * 2
+
+
+def scatter_head(blocks, tag):
+    parts, rows, width = blocks.shape
+
+    def body(*refs):
+        pair_scatter(8, *refs)
+
+    return pl.pallas_call(
+        body,
+        out_shape=jax.ShapeDtypeStruct((rows, width), jnp.float32),
+        in_specs=[pl.BlockSpec(memory_space=pltpu.VMEM)],
+        out_specs=pl.BlockSpec(memory_space=pltpu.VMEM),
+        scratch_shapes=[
+            pltpu.VMEM((2, rows, width), blocks.dtype),
+            pltpu.VMEM((rows, width), blocks.dtype),
+        ]
+        + pair_sems(8),
+        compiler_params=pltpu.CompilerParams(collective_id=tag, has_side_effects=True),
+        name="pair_scatter",
+    )(blocks)
+
+
+def gather_head(block, tag):
+    def body(*refs):
+        pair_gather(8, *refs)
+
+    return pl.pallas_call(
+        body,
+        out_shape=jax.ShapeDtypeStruct((4,) + block.shape, block.dtype),
+        in_specs=[pl.BlockSpec(memory_space=pltpu.VMEM)],
+        out_specs=pl.BlockSpec(memory_space=pltpu.VMEM),
+        scratch_shapes=pair_sems(8) + [pltpu.SemaphoreType.DMA],
+        compiler_params=pltpu.CompilerParams(collective_id=tag, has_side_effects=True),
+        name="pair_gather",
+    )(block)
+
+
 def dense_device(queries, keys, values, w_in, w_out, routes, route_weights, grad_out):
     exp_count = lax.axis_size("exp")
     exp_index = lax.axis_index("exp")
@@ -422,24 +555,18 @@
     back_sums = jnp.einsum(
         "rd,hfd->hrf", grads, second_split, preferred_element_type=jnp.float32
     ).astype(jnp.bfloat16)
-    back_value = lax.psum_scatter(back_sums, "head", scatter_dimension=0, tiled=False)
     row_float = rows.astype(jnp.float32)
     raw_sums = jnp.einsum("rd,dkhf->hrkf", rows, w_split, preferred_element_type=jnp.float32)
     raw_sums = raw_sums.astype(jnp.bfloat16).reshape(parts, count, 2 * share)
     squares = jnp.sum(row_float * row_float, axis=1)
     square_tile = jnp.broadcast_to(
-        squares.astype(jnp.bfloat16)[None, :, None], (parts, count, 128)
-    )
-    raw_part = lax.psum_scatter(
-        jnp.concatenate([raw_sums, square_tile], axis=2),
-        "head",
-        scatter_dimension=0,
-        tiled=False,
-    ).astype(jnp.float32)
-    norm_scale = lax.rsqrt(raw_part[:, 2 * share : 2 * share + 1] / D + norm_eps)
+        squares.astype(jnp.bfloat16)[None, :, None], (parts, count, -3 * share % 128 + 128 * (share * 3 % 128 == 0))
+    )
+    raw_part = scatter_head(jnp.concatenate([raw_sums, back_sums, square_tile], axis=2), 4)
+    norm_scale = lax.rsqrt(raw_part[:, 3 * share : 3 * share + 1] / D + norm_eps)
     gate_value = raw_part[:, :share] * norm_scale
     up_value = raw_part[:, share : 2 * share] * norm_scale
-    back_value = back_value.astype(jnp.float32)
+    back_value = raw_part[:, 2 * share : 3 * share]
     sigmoid = jax.nn.sigmoid(gate_value)
     silu = gate_value * sigmoid
     act = (silu * up_value).astype(jnp.bfloat16)
@@ -454,7 +581,7 @@
     )
     sent = jnp.concatenate([act, grad_gate, grad_up, *three_parts(inner)], axis=1)
     sent = jnp.pad(sent, ((0, 0), (0, -sent.shape[1] % 128)))
-    whole = lax.all_gather(sent, "head", axis=0, tiled=False)
+    whole = gather_head(sent, 5)
     inner_sum = jnp.sum(whole[:, :, 3 * share : 3 * share + 3].astype(jnp.float32), axis=(0, 2))[
         :, None
     ]
@@ -485,7 +612,7 @@
 
 
 def solution(mesh):
-    dense = 2 * TOP >= mesh.shape["exp"] and mesh.shape["exp"] % 2 == 0
+    dense = 2 * TOP >= mesh.shape["exp"] and mesh.shape["exp"] % 2 == 0 and mesh.shape["head"] == 4
     in_specs = (
         P("exp", "head"),
         P("exp", "head"),

time: 308 us -> 284 us (0.922)
  waiting for transfers between devices: 101 us -> 0 us
  Pallas kernels: 117 us -> 189 us
  between operations: 14 us -> 0.84 us
  local copies, waits for them, and re-layouts: 36.6 us -> 46.5 us
  other arithmetic: 20 us -> 26.1 us
    pallas_call x0 -> x2, Pallas kernels: none -> 72.8 us  [the longest x1 36.9 us: scatter_head(): pl.pallas_call(body, out_shape=jax.ShapeDtypeStruct((rows, width), jnp.fl...]
    reduce_scatter x2 -> x0, waiting for transfers between devices: 66.1 us -> none  [the longest x1 38.9 us: dense_device(): lax.psum_scatter(jnp.concatenate([raw_sums, square_tile], axis=2), 'head'...]
    all_gather x1 -> x0, waiting for transfers between devices: 35.1 us -> none  [dense_device(): whole = lax.all_gather(sent, 'head', axis=0, tiled=False)]
    transpose x0 -> x4, local copies, waits for them, and re-layouts: none -> 16.8 us  [the longest x2 9.93 us: dense_device(): jnp.transpose(whole[:, :, :share], (1, 0, 2)).reshape(count, hidden)]
    all_gather x1 -> x0, local copies, waits for them, and re-layouts: 9.49 us -> none  [dense_device(): whole = lax.all_gather(sent, 'head', axis=0, tiled=False)]
    reshape x0 -> x1, local copies, waits for them, and re-layouts: none -> 4.69 us  [dense_device(): raw_sums = raw_sums.astype(jnp.bfloat16).reshape(parts, count, 2 * share)]
    concatenate x1, other arithmetic: 2.38 us -> 7.06 us  [dense_device(): jnp.concatenate([raw_sums, back_sums, square_tile], axis=2)]
    unnamed x23 -> x12, local copies, waits for them, and re-layouts: 16.3 us -> 12.4 us
  transfers between devices with their start and end apart: 3 -> 0, of which waited for: 3 -> 0; matrix products, arithmetic and copies ran while one was open for 4% -> 0% of each run, Pallas kernels for 0% -> 0%
where the time goes in v3:
time: 284 us; the launch traced here: 283 us
  Pallas kernels  189 us (67%)
  local copies, waits for them, and re-layouts  46.5 us (16%)
  other arithmetic  26.1 us (9%)
  matrix products  20.1 us (7%)
    pallas_call x2, Pallas kernels, gather_exp(): pl.pallas_call(gather_body, out_shape=jax.ShapeDtypeStruct((count * rows,...  65.3 us
    pallas_call x1, Pallas kernels, scatter_exp(): pl.pallas_call(scatter_body, out_shape=jax.ShapeDtypeStruct((rows, width)...  46 us
    pallas_call x1, Pallas kernels, scatter_head(): pl.pallas_call(body, out_shape=jax.ShapeDtypeStruct((rows, width), jnp.fl...  36.9 us
    pallas_call x1, Pallas kernels, gather_head(): pl.pallas_call(body, out_shape=jax.ShapeDtypeStruct((4,) + block.shape, b...  35.9 us
    unnamed x12, local copies, waits for them, and re-layouts  12.4 us
    transpose x2, local copies, waits for them, and re-layouts, dense_device(): jnp.transpose(whole[:, :, :share], (1, 0, 2)).reshape(count, hidden)  9.93 us
    dot_general x1, matrix products, dense_device(): lax.dot_general(grad_all, w_first.reshape(width, 2 * hidden), (((1,), (1,...  7.41 us
    concatenate x1, other arithmetic, dense_device(): jnp.concatenate([raw_sums, back_sums, square_tile], axis=2)  7.06 us

profile of v3, /device:TPU:0, one launch (start us, length us, event | category | flops | bytes accessed | tf_op | source)
XLA Modules:
  0.0 282.6 jit_solution(6665332833347409613)
XLA Ops:
  0.6 1.4 copy-done
  2.9 1.8 fusion.21.refs_0_
  4.7 40.3 %ring_gather_1.1 = bf16[1024,1664]{1,0:T(8,128)(2,1)} custom-call(bf16[128,1664]{1,0:T(8,128)(2,1)} %fusion.21.refs_0_), custom_call_target="tpu_custom_call" | custom-call | tf_op jit(solution)/shard_map/ring_gather_1/pallas_call | solution.py:362
  44.9 1.0 slice_convert_fusion
  46.2 2.3 fusion.25
  48.5 3.4 %fusion.15 = bf16[1024,4,192]{0,2,1:T(8,128)(2,1)S(1)} fusion(bf16[4,192,1024]{2,1,0:T(8,128)(2,1)S(1)} %bitcast.39, bf16[1024,1664]{1,0:T(8,128)(2,1)} %ring_gather_1.1), kind=kOutput, calls=%fused_computation.23 | convolution fusion | flops 1611399168 | bytes 5242880 | tf_op jit(solution)/shard_map/rd,hfd->hrf/dot_general | solution.py:555
  51.9 5.0 %attention.1.refs_0_ = bf16[128,1024]{1,0:T(8,128)(2,1)} custom-call(s32[1]{0:T(128)} %bitcast.refs_0_, bf16[128,1024]{1,0:T(8,128)(2,1)} %refs_1_.1, bf16[1024,256]{1,0:T(8,128)(2,1)} %get-tuple-element.11.refs_2_, bf16[1024,256]{1,0:T(8,128)(2,1)} %get-tuple-element.10.refs_3_), custom_call_target="tpu_custom_call" | custom-call | tf_op jit(solution)/shard_map/attention/pallas_call | solution.py:220
  56.9 2.5 copy.63
  59.4 25.0 %ring_gather_2.1 = bf16[1024,1024]{1,0:T(8,128)(2,1)} custom-call(bf16[128,1024]{1,0:T(8,128)(2,1)} %attention.1.refs_0_), custom_call_target="tpu_custom_call" | custom-call | tf_op jit(solution)/shard_map/ring_gather_2/pallas_call | solution.py:362
  84.4 2.2 fusion
  86.9 2.3 copy.75
  89.2 8.7 %copy.61 = bf16[1,1024,2,768]{1,3,2,0:T(8,128)(2,1)} copy(bf16[1,1024,2,768]{3,2,1,0:T(2,128)(2,1)} %param.11) | data formatting | bytes 6291456 | tf_op args[3]
  97.9 6.0 %fusion.27 = f32[1024,1536]{0,1:S(1)} fusion(bf16[1024,1024]{1,0:T(8,128)(2,1)} %ring_gather_2.1, bf16[1024,1536]{0,1:T(8,128)(2,1)} %bitcast.46), kind=kOutput, calls=%fused_computation.58 | convolution fusion | flops 3221225472 | bytes 11534336
  104.4 2.0 copy.62
  106.4 4.7 %copy.64 = bf16[4,1024,384]{2,1,0:T(8,128)(2,1)} copy(bf16[4,1024,384]{1,2,0:T(8,128)(2,1)} %bitcast.42) | data formatting | bytes 6291456 | tf_op jit(solution)/shard_map/reshape | solution.py:560
  111.1 7.1 %pad_maximum_fusion.refs_0_ = bf16[4,1024,640]{2,1,0:T(8,128)(2,1)} fusion(bf16[4,1024,64]{2,1,0:T(8,128)(2,1)S(1)} %broadcast_in_dim.44, bf16[4,1024,192]{2,1,0:T(8,128)(2,1)} %bitcast.43, bf16[4,1024,384]{2,1,0:T(8,128)(2,1)} %copy.64), kind=kLoop, calls=%fused_computation.2 | loop fusion | flops 15728640 | bytes 10485760 | tf_op jit(solution)/shard_map/concatenate | solution.py:565
  118.2 36.9 %pair_scatter.1 = f32[1024,640]{1,0:T(8,128)} custom-call(bf16[4,1024,640]{2,1,0:T(8,128)(2,1)} %pad_maximum_fusion.refs_0_), custom_call_target="tpu_custom_call" | custom-call | tf_op jit(solution)/shard_map/pair_scatter/pallas_call | solution.py:494
  155.1 1.5 multiply_reduce_fusion
  156.6 4.0 %add_reduce_fusion = (f32[1024]{0:T(1024)S(1)}, bf16[1024,192]{1,0:T(8,128)(2,1)S(1)}, bf16[1024,192]{1,0:T(8,128)(2,1)}, bf16[1024,192]{1,0:T(8,128)(2,1)}) fusion(f32[1024,640]{1,0:T(8,128)} %pair_scatter.1, f32[1024]{0:T(1024)S(1)} %get-tuple-element.3), kind=kLoop, calls=%fused_computation.25 | loop fusion | flops 4520960 | bytes 3547136 | tf_op jit(solution)/shard_map/reduce_sum | solution.py:577
  162.9 2.8 concatenate.21
  165.7 1.2 pad.9.refs_0_
  166.9 35.9 %pair_gather.1 = bf16[4,1024,640]{2,1,0:T(8,128)(2,1)} custom-call(bf16[1024,640]{1,0:T(8,128)(2,1)} %pad.9.refs_0_), custom_call_target="tpu_custom_call" | custom-call | tf_op jit(solution)/shard_map/pair_gather/pallas_call | solution.py:513
  202.8 1.8 convert_reduce_fusion
  204.6 7.0 %slice_bitcast_fusion.2 = (bf16[1024,4,192]{2,0,1:T(8,128)(2,1)}, bf16[1024,4,192]{2,0,1:T(8,128)(2,1)}, bf16[1024,4,192]{2,0,1:T(8,128)(2,1)}) fusion(bf16[4,1024,640]{2,1,0:T(8,128)(2,1)} %pair_gather.1), kind=kLoop, calls=%fused_computation.21 | loop fusion | bytes 9437184 | tf_op jit(solution)/shard_map/transpose | solution.py:588
  211.6 2.9 %copy.68 = bf16[1024,4,192]{0,2,1:T(8,128)(2,1)S(1)} copy(bf16[1024,4,192]{2,0,1:T(8,128)(2,1)} %get-tuple-element.7) | data formatting | bytes 3145728 | tf_op jit(solution)/shard_map/transpose | solution.py:588
  214.5 3.2 %select_convert_fusion = bf16[1024,1024]{1,0:T(8,128)(2,1)} fusion(bf16[1024,768]{0,1:T(8,128)(2,1)S(1)} %bitcast.49, f32[1024]{0:T(1024)S(1)} %multiply_reduce_fusion.1, pred[1024]{0:T(1024)(128)(4,1)S(1)} %broadcast_compare_fusion, bf16[1,768,1024]{2,1,0:T(8,128)(2,1)S(1)} %copy-done), kind=kOutput, calls=%fused_computation.10 | convolution fusion | flops 1613758464 | bytes 5248000 | tf_op jit(solution)/shard_map/dot_general | solution.py:592
  217.7 2.9 %copy.71 = bf16[1024,4,192]{0,2,1:T(8,128)(2,1)S(1)} copy(bf16[1024,4,192]{2,0,1:T(8,128)(2,1)} %get-tuple-element.8) | data formatting | bytes 3145728 | tf_op jit(solution)/shard_map/transpose | solution.py:590
  220.7 3.9 %copy.70 = bf16[1024,4,192]{0,2,1:T(8,128)(2,1)} copy(bf16[1024,4,192]{2,0,1:T(8,128)(2,1)} %get-tuple-element.9) | data formatting | bytes 3145728 | tf_op jit(solution)/shard_map/transpose | solution.py:589
  224.6 7.4 %fusion.5 = bf16[1024,1024]{1,0:T(8,128)(2,1)S(1)} fusion(bf16[1024,1024]{1,0:T(8,128)(2,1)} %ring_gather_2.1, bf16[1024,1536]{1,0:T(8,128)(2,1)} %bitcast.45, bf16[1024,768]{0,1:T(8,128)(2,1)S(1)} %bitcast.47, bf16[1024,768]{0,1:T(8,128)(2,1)} %bitcast.48, f32[1024]{0:T(1024)S(1)} %convert_reduce_fusion, f32[1024]{0:T(1024)S(1)} %get-tuple-element.2, ...), kind=kOutput, calls=%fused_computation.8 | convolution fusion | flops 3235905536 | bytes 10503168 | tf_op jit(solution)/shard_map/dot_general | solution.py:593
  232.0 2.4 pad_maximum_fusion.1
  234.4 46.0 %ring_scatter.1 = f32[128,2048]{1,0:T(8,128)} custom-call(bf16[8,128,2048]{2,1,0:T(8,128)(2,1)} %bitcast.40), custom_call_target="tpu_custom_call" | custom-call | tf_op jit(solution)/shard_map/ring_scatter/pallas_call | solution.py:379
  280.5 2.1 add_convert_fusion
  (26 shorter events, 4.1 us)
Async XLA Ops:
  0.6 1.4 copy-start
  84.4 2.5 copy-start.1
  224.6 7.4 %copy-start.3 = (bf16[1024,1024]{1,0:T(8,128)(2,1)S(1)}, bf16[1024,1024]{1,0:T(8,128)(2,1)}, u32[]{:S(2)}) copy-start(bf16[1024,1024]{1,0:T(8,128)(2,1)} %select_convert_fusion) | copy-start | bytes 6291460
  234.4 46.0 %copy-start.2 = (bf16[128,1024]{1,0:T(8,128)(2,1)S(1)}, bf16[128,1024]{1,0:T(8,128)(2,1)}, u32[]{:S(2)}) copy-start(bf16[128,1024]{1,0:T(8,128)(2,1)} %attention.1.refs_0_) | copy-start | bytes 786436
  234.4 46.0 %copy-start.4 = (bf16[128,1024]{1,0:T(8,128)(2,1)S(1)}, bf16[128,1024]{1,0:T(8,128)(2,1)}, u32[]{:S(2)}) copy-start(bf16[128,1024]{1,0:T(8,128)(2,1)} %param.15) | copy-start | bytes 786436

commit v4 on v3

--- a/solution.py
+++ b/solution.py
@@ -585,16 +585,12 @@
     inner_sum = jnp.sum(whole[:, :, 3 * share : 3 * share + 3].astype(jnp.float32), axis=(0, 2))[
         :, None
     ]
-    act_all = jnp.transpose(whole[:, :, :share], (1, 0, 2)).reshape(count, hidden)
-    gate_all = jnp.transpose(whole[:, :, share : 2 * share], (1, 0, 2)).reshape(count, hidden)
-    up_all = jnp.transpose(whole[:, :, 2 * share : 3 * share], (1, 0, 2)).reshape(count, hidden)
-    grad_all = jnp.concatenate([gate_all, up_all], axis=1)
-    out_rows = jnp.dot(act_all, w_second, preferred_element_type=jnp.float32)
-    grad_normed = lax.dot_general(
-        grad_all,
-        w_first.reshape(width, 2 * hidden),
-        (((1,), (1,)), ((), ())),
-        preferred_element_type=jnp.float32,
+    out_rows = jnp.einsum(
+        "hrf,hfd->rd", whole[:, :, :share], second_split, preferred_element_type=jnp.float32
+    )
+    grad_pair = whole[:, :, share : 3 * share].reshape(parts, count, 2, share)
+    grad_normed = jnp.einsum(
+        "hrkf,dkhf->rd", grad_pair, w_split, preferred_element_type=jnp.float32
     )
     grad_rows = norm_scale * grad_normed - row_float * (norm_scale * norm_scale / D) * inner_sum
     routed = gain > 0.0

time: 284 us -> 275 us (0.968)
  local copies, waits for them, and re-layouts: 46.5 us -> 35.7 us
    transpose x4 -> x0, local copies, waits for them, and re-layouts: 16.8 us -> none  [the longest x2 9.93 us: dense_device(): jnp.transpose(whole[:, :, :share], (1, 0, 2)).reshape(count, hidden)]
    slice x0 -> x2, local copies, waits for them, and re-layouts: none -> 8.23 us  [dense_device(): grad_pair = whole[:, :, share:3 * share].reshape(parts, count, 2, share)]
    unnamed x12 -> x13, local copies, waits for them, and re-layouts: 12.4 us -> 10.2 us
where the time goes in v4:
time: 275 us; the launch traced here: 274 us
  Pallas kernels  189 us (69%)
  local copies, waits for them, and re-layouts  35.7 us (13%)
  other arithmetic  26.1 us (9%)
  matrix products  22 us (8%)
    pallas_call x2, Pallas kernels, gather_exp(): pl.pallas_call(gather_body, out_shape=jax.ShapeDtypeStruct((count * rows,...  65.4 us
    pallas_call x1, Pallas kernels, scatter_exp(): pl.pallas_call(scatter_body, out_shape=jax.ShapeDtypeStruct((rows, width)...  46 us
    pallas_call x1, Pallas kernels, scatter_head(): pl.pallas_call(body, out_shape=jax.ShapeDtypeStruct((rows, width), jnp.fl...  37 us
    pallas_call x1, Pallas kernels, gather_head(): pl.pallas_call(body, out_shape=jax.ShapeDtypeStruct((4,) + block.shape, b...  35.8 us
    unnamed x13, local copies, waits for them, and re-layouts  10.2 us
    slice x2, local copies, waits for them, and re-layouts, dense_device(): grad_pair = whole[:, :, share:3 * share].reshape(parts, count, 2, share)  8.23 us
    dot_general x1, matrix products, dense_device(): jnp.einsum('hrkf,dkhf->rd', grad_pair, w_split, preferred_element_type=jn...  7.8 us
    concatenate x1, other arithmetic, dense_device(): jnp.concatenate([raw_sums, back_sums, square_tile], axis=2)  7.07 us

profile of v4, /device:TPU:0, one launch (start us, length us, event | category | flops | bytes accessed | tf_op | source)
XLA Modules:
  0.0 273.8 jit_solution(6819566176959338351)
XLA Ops:
  0.7 1.4 copy-done
  2.0 0.7 select_reduce_fusion
  2.9 1.8 fusion.21.refs_0_
  4.7 40.3 %ring_gather_1.1 = bf16[1024,1664]{1,0:T(8,128)(2,1)} custom-call(bf16[128,1664]{1,0:T(8,128)(2,1)} %fusion.21.refs_0_), custom_call_target="tpu_custom_call" | custom-call | tf_op jit(solution)/shard_map/ring_gather_1/pallas_call | solution.py:362
  44.9 1.0 slice_convert_fusion
  46.2 2.3 fusion.24
  48.5 3.4 %fusion.16 = bf16[1024,4,192]{0,2,1:T(8,128)(2,1)S(1)} fusion(bf16[4,192,1024]{2,1,0:T(8,128)(2,1)S(1)} %bitcast.35, bf16[1024,1664]{1,0:T(8,128)(2,1)} %ring_gather_1.1), kind=kOutput, calls=%fused_computation.22 | convolution fusion | flops 1611399168 | bytes 5242880 | tf_op jit(solution)/shard_map/rd,hfd->hrf/dot_general | solution.py:555
  51.9 5.0 %attention.1.refs_0_ = bf16[128,1024]{1,0:T(8,128)(2,1)} custom-call(s32[1]{0:T(128)} %bitcast.refs_0_, bf16[128,1024]{1,0:T(8,128)(2,1)} %refs_1_.1, bf16[1024,256]{1,0:T(8,128)(2,1)} %get-tuple-element.8.refs_2_, bf16[1024,256]{1,0:T(8,128)(2,1)} %get-tuple-element.7.refs_3_), custom_call_target="tpu_custom_call" | custom-call | tf_op jit(solution)/shard_map/attention/pallas_call | solution.py:220
  56.9 2.5 copy.66
  59.4 25.1 %ring_gather_2.1 = bf16[1024,1024]{1,0:T(8,128)(2,1)} custom-call(bf16[128,1024]{1,0:T(8,128)(2,1)} %attention.1.refs_0_), custom_call_target="tpu_custom_call" | custom-call | tf_op jit(solution)/shard_map/ring_gather_2/pallas_call | solution.py:362
  84.4 2.1 fusion
  86.7 8.8 %copy.64 = bf16[1,1024,2,768]{1,3,2,0:T(8,128)(2,1)} copy(bf16[1,1024,2,768]{3,2,1,0:T(2,128)(2,1)} %param.11) | data formatting | bytes 6291456 | tf_op args[3]
  95.5 6.0 %fusion.26 = f32[1024,1536]{0,1:S(1)} fusion(bf16[1024,1024]{1,0:T(8,128)(2,1)} %ring_gather_2.1, bf16[1024,1536]{0,1:T(8,128)(2,1)} %bitcast.43), kind=kOutput, calls=%fused_computation.55 | convolution fusion | flops 3221225472 | bytes 11534336
  102.0 2.0 copy.65
  104.0 4.7 %copy.67 = bf16[4,1024,384]{2,1,0:T(8,128)(2,1)} copy(bf16[4,1024,384]{1,2,0:T(8,128)(2,1)} %bitcast.40) | data formatting | bytes 6291456 | tf_op jit(solution)/shard_map/reshape | solution.py:560
  108.7 7.1 %pad_maximum_fusion.refs_0_ = bf16[4,1024,640]{2,1,0:T(8,128)(2,1)} fusion(bf16[4,1024,64]{2,1,0:T(8,128)(2,1)S(1)} %broadcast_in_dim.44, bf16[4,1024,192]{2,1,0:T(8,128)(2,1)} %bitcast.41, bf16[4,1024,384]{2,1,0:T(8,128)(2,1)} %copy.67), kind=kLoop, calls=%fused_computation.2 | loop fusion | flops 15728640 | bytes 10485760 | tf_op jit(solution)/shard_map/concatenate | solution.py:565
  115.8 37.0 %pair_scatter.1 = f32[1024,640]{1,0:T(8,128)} custom-call(bf16[4,1024,640]{2,1,0:T(8,128)(2,1)} %pad_maximum_fusion.refs_0_), custom_call_target="tpu_custom_call" | custom-call | tf_op jit(solution)/shard_map/pair_scatter/pallas_call | solution.py:494
  152.7 1.5 multiply_reduce_fusion
  154.3 4.0 %add_reduce_fusion = (f32[1024]{0:T(1024)S(1)}, bf16[1024,192]{1,0:T(8,128)(2,1)S(1)}, bf16[1024,192]{1,0:T(8,128)(2,1)}, bf16[1024,192]{1,0:T(8,128)(2,1)}) fusion(f32[1024,640]{1,0:T(8,128)} %pair_scatter.1, f32[1024]{0:T(1024)S(1)} %get-tuple-element.3), kind=kLoop, calls=%fused_computation.23 | loop fusion | flops 4520960 | bytes 3547136 | tf_op jit(solution)/shard_map/reduce_sum | solution.py:577
  158.3 0.9 copy.70
  159.6 0.9 subtract_convert_fusion
  160.6 2.8 %concatenate.18 = bf16[1024,579]{1,0:T(8,128)(2,1)S(1)} concatenate(bf16[1024,192]{1,0:T(8,128)(2,1)} %get-tuple-element.9, bf16[1024,192]{1,0:T(8,128)(2,1)} %get-tuple-element.6, bf16[1024,192]{1,0:T(8,128)(2,1)S(1)} %get-tuple-element.5, bf16[1024,1]{1,0:T(8,128)(2,1)} %copy.70, bf16[1024,1]{1,0:T(8,128)(2,1)} %get-tuple-element.13, bf16[1024,1]{1,0:T(8,128)(2,1)} %get-tuple-element.12), dimensions={1} | concatenate | bytes 2371584 | tf_op jit(solution)/shard_map/concatenate | solution.py:582
  163.3 1.3 pad.9.refs_0_
  164.6 35.8 %pair_gather.1 = bf16[4,1024,640]{2,1,0:T(8,128)(2,1)} custom-call(bf16[1024,640]{1,0:T(8,128)(2,1)} %pad.9.refs_0_), custom_call_target="tpu_custom_call" | custom-call | tf_op jit(solution)/shard_map/pair_gather/pallas_call | solution.py:513
  200.4 1.9 convert_reduce_fusion
  202.4 4.8 %fusion.7 = bf16[1024,1024]{1,0:T(8,128)(2,1)} fusion(bf16[4,192,1024]{2,1,0:T(8,128)(2,1)S(1)} %bitcast.36, bf16[4,1024,640]{2,1,0:T(8,128)(2,1)} %pair_gather.1, f32[1024]{0:T(1024)S(1)} %multiply_reduce_fusion.1, pred[1024]{0:T(1024)(128)(4,1)S(1)} %broadcast_compare_fusion), kind=kOutput, calls=%fused_computation.13 | convolution fusion | flops 1613758464 | bytes 5772288 | tf_op jit(solution)/shard_map/hrf,hfd->rd/dot_general | solution.py:588
  207.2 3.6 %slice.54 = bf16[4,1024,384]{2,1,0:T(8,128)(2,1)} slice(bf16[4,1024,640]{2,1,0:T(8,128)(2,1)S(1)} %bitcast.38), slice={[0:4], [0:1024], [192:576]} | slice | bytes 6291456 | tf_op jit(solution)/shard_map/slice | solution.py:591
  210.8 4.6 %copy.73 = bf16[4,1024,384]{1,2,0:T(8,128)(2,1)} copy(bf16[4,1024,384]{2,1,0:T(8,128)(2,1)} %slice.54) | data formatting | bytes 6291456 | tf_op jit(solution)/shard_map/slice | solution.py:591
  215.4 7.8 %fusion.5 = bf16[1024,1024]{1,0:T(8,128)(2,1)S(1)} fusion(bf16[1024,1024]{1,0:T(8,128)(2,1)} %ring_gather_2.1, bf16[4,1024,2,192]{1,3,2,0:T(8,128)(2,1)} %bitcast.45, bf16[1024,2,4,192]{0,3,2,1:T(8,128)(2,1)} %bitcast.44, f32[1024]{0:T(1024)S(1)} %convert_reduce_fusion, f32[1024]{0:T(1024)S(1)} %get-tuple-element.2, f32[1024]{0:T(1024)S(1)} %get-tuple-element.3, ...), kind=kOutput, calls=%fused_computation.8 | convolution fusion | flops 3229614080 | bytes 10503168 | tf_op jit(solution)/shard_map/hrkf,dkhf->rd/dot_general | solution.py:592
  223.3 2.4 pad_maximum_fusion.1
  225.6 46.0 %ring_scatter.1 = f32[128,2048]{1,0:T(8,128)} custom-call(bf16[8,128,2048]{2,1,0:T(8,128)(2,1)} %bitcast.39), custom_call_target="tpu_custom_call" | custom-call | tf_op jit(solution)/shard_map/ring_scatter/pallas_call | solution.py:379
  271.7 2.1 add_convert_fusion
  (26 shorter events, 1.6 us)
Async XLA Ops:
  0.6 1.4 copy-start
  200.4 6.8 %slice-start = ((s8[5242880]{0:T(1024)(128)(4,1)}), s8[4194304]{0:T(1024)(128)(4,1)S(1)}, s32[]{:S(2)}) async-start(s8[5242880]{0:T(1024)(128)(4,1)} %bitcast.37), calls=%async_computation | async-start | bytes 8388608
  202.4 4.8 %slice-start.1 = ((s8[5242880]{0:T(1024)(128)(4,1)}), s8[1048576]{0:T(1024)(128)(4,1)S(1)}, s32[]{:S(2)}) async-start(s8[5242880]{0:T(1024)(128)(4,1)} %bitcast.37), calls=%async_computation.1 | async-start | bytes 2097152
  215.4 7.8 %copy-start.2 = (bf16[1024,1024]{1,0:T(8,128)(2,1)S(1)}, bf16[1024,1024]{1,0:T(8,128)(2,1)}, u32[]{:S(2)}) copy-start(bf16[1024,1024]{1,0:T(8,128)(2,1)} %fusion.7) | copy-start | bytes 6291460
  225.6 46.0 %copy-start.1 = (bf16[128,1024]{1,0:T(8,128)(2,1)S(1)}, bf16[128,1024]{1,0:T(8,128)(2,1)}, u32[]{:S(2)}) copy-start(bf16[128,1024]{1,0:T(8,128)(2,1)} %attention.1.refs_0_) | copy-start | bytes 786436
  225.6 46.0 %copy-start.3 = (bf16[128,1024]{1,0:T(8,128)(2,1)S(1)}, bf16[128,1024]{1,0:T(8,128)(2,1)}, u32[]{:S(2)}) copy-start(bf16[128,1024]{1,0:T(8,128)(2,1)} %param.15) | copy-start | bytes 786436
